TPU v7x, 32 devices: a whole 2x2x4 slice. The times are simulated.
32 devices in a mesh: dp: 2 (over y), expert: 16 (over z, x, core).
Axes of the slice: x: 2, y: 2, z: 4, core: 2. Of those that a mesh axis runs over, the one named last changes fastest.
Arguments:
- tokens: bfloat16 [4096, 2048], P(('dp', 'expert')), may hold values from -6 to 6
- cotangent: bfloat16 [4096, 2048], P(('dp', 'expert')), may hold values from -6 to 6
- gate_probs: float32 [4096, 2], P(('dp', 'expert')), may hold values from 0.2 to 1
- expert_ids: int32 [4096, 2], P(('dp', 'expert')), may hold values from 0 to 15, as said below
- route_slots: int32 [4096, 2], P(('dp', 'expert')), may hold values from 0 to 4, as said below
- hot_mask: int32 [16], replicated, may hold values from 0 to 1, as said below
- w_up: bfloat16 [16, 2048, 4096], P('expert', None, 'dp'), may hold values from -0.125 to 0.125
- w_down: bfloat16 [16, 4096, 2048], P('expert', 'dp'), may hold values from -0.09375 to 0.09375
Outputs:
- layer_out: bfloat16 [4096, 2048], P(('dp', 'expert'))
- grad_tokens: bfloat16 [4096, 2048], P(('dp', 'expert'))
- grad_up: bfloat16 [16, 2048, 4096], P(None, 'expert', 'dp')
- grad_down: bfloat16 [16, 2048, 4096], P(None, 'expert', 'dp')
Inputs may be any that keep to these rules, and one draw needn't show every extreme that they name: `expert_ids`: A token's two experts differ. Only first choices name the hot expert. Every device's 128 tokens (aligned blocks) name the hot expert at least 4 + 1 times. route_slots[t, c] is the rank of route (t, c) among the routes of the same device's 128 tokens (aligned blocks) to the same expert, counting all first choices in token order before all second choices, capped at 4. `hot_mask`: exactly one entry is 1.
All inputs are finite; a program needn't handle non-finite values.
Results may differ from a plain program's by a relative error of at most 0.014.
Values may be sent and summed in bfloat16 or wider, within the bound.
No kernel may reach another device: no remote copies, remote signals or barrier semaphores. Data moves between devices by JAX's collectives and lax.ppermute only.
A program may use at most 128 MiB of HBM per device.

v0:
```python
import functools

import jax
import jax.numpy as jnp
from jax import lax
from jax.experimental import pallas as pl
from jax.experimental.pallas import tpu as pltpu
from jax.sharding import PartitionSpec as P


CAP = 2
HCAP = 4
EXTRA = HCAP - CAP
BF16 = jnp.bfloat16
F32 = jnp.float32


def in_vmem(value):
    return pltpu.with_memory_space_constraint(value, pltpu.VMEM)


def in_hbm(value):
    return pltpu.with_memory_space_constraint(value, pltpu.HBM)


def gelu_pair(preact):
    normal_cdf = 0.5 * (1.0 + lax.erf(preact * 0.7071067811865476))
    density = jnp.exp(-0.5 * preact * preact) * 0.3989422804014327
    return (preact * normal_cdf, normal_cdf + preact * density)


def matmul(left, right):
    return jnp.dot(left, right, preferred_element_type=F32)


def chip_ring(device_count):
    chips = device_count // 2
    half = chips // 2
    return [2 * i for i in range(half)] + [2 * i + 1 for i in reversed(range(chips - half))]


def ring_pairs(device_count, shift):
    ring = chip_ring(device_count)
    size = len(ring)
    return [
        (2 * ring[k] + core, 2 * ring[(k + shift) % size] + core)
        for k in range(size)
        for core in range(2)
    ]


def send(value, pairs):
    return lax.ppermute(value, "expert", pairs)


def dp_shift(value, shift):
    count = lax.axis_size("dp")
    return lax.ppermute(value, "dp", [(p, (p + shift) % count) for p in range(count)])


def gather_planes(own):
    count = lax.axis_size("dp")
    return [own] + [dp_shift(own, -shift) for shift in range(1, count)]


def sum_planes(blocks):
    count = lax.axis_size("dp")
    total = blocks[0].astype(F32)
    for shift in range(1, count):
        total = total + dp_shift(blocks[shift], shift).astype(F32)
    return total.astype(BF16)


def flip_bit(device_count, bit):
    return [(i, i ^ bit) for i in range(device_count)]


def ring_gather(value):
    count = lax.axis_size("expert")
    size = count // 2
    right, left = ring_pairs(count, 1), ring_pairs(count, -1)
    got = {0: [value]}
    going_right = going_left = value
    for step in range(1, (size - 1) // 2 + 1):
        going_right = send(going_right, right)
        going_left = send(going_left, left)
        got[-step], got[step] = [going_right], [going_left]
    if size % 2 == 0:
        half = value.shape[0] // 2
        far_right = send(going_right[:half], right)
        far_left = send(going_left[half:], left)
        got[-(size // 2)] = [far_right, far_left]
    return got


def ring_groups(count):
    size = count // 2
    groups = [[0]] + [[-step, step] for step in range(1, (size - 1) // 2 + 1)]
    return groups + ([[-(size // 2)]] if size % 2 == 0 else [])


def ring_sources(count):
    size = count // 2
    half = size // 2
    index = lax.axis_index("expert")
    chip, core = index // 2, index % 2
    place = jnp.where(chip % 2 == 0, chip // 2, size - 1 - chip // 2)
    groups = ring_groups(count)
    distances = jnp.array([d for group in groups for d in group * 2], dtype=jnp.int32)
    other = jnp.array(
        [o for group in groups for o in [0] * len(group) + [1] * len(group)], dtype=jnp.int32
    )
    there = lax.rem(place + distances + size, size)
    chip_there = jnp.where(there < half, 2 * there, 2 * (size - 1 - there) + 1)
    return 2 * chip_there + jnp.where(other == 1, 1 - core, core)


def grad_body(layout, first, ids_ref, cols_ref, *refs):
    del ids_ref
    blocks = sum(layout)
    up_ref, down_ref = refs[blocks + (0 if first else 2) :]
    width = cols_ref.shape[2] // 2
    rows = cols_ref.shape[1]
    dims = (((0,), (0,)), ((), ()))
    step = pl.program_id(0)
    at = 0
    for k, parts in enumerate(layout):
        if parts == 1:
            act, dpre = refs[at].at[:rows], refs[at].at[rows:]
        else:
            act, dpre = refs[at], refs[at + 1]
        at += parts

        @pl.when(step == k)
        def _(act=act, dpre=dpre):
            up = lax.dot_general(
                cols_ref[0, :, :width], dpre[...], dims, preferred_element_type=F32
            )
            up_ref[0] = up.astype(BF16)
            down = lax.dot_general(
                cols_ref[0, :, width:], act[...], dims, preferred_element_type=F32
            )
            down_ref[0] = down.astype(BF16)


def grad_stage(ids, at, cols, chunks, totals, out_shape):
    group = len(chunks)
    first = totals is None
    layout = [len(chunk) for chunk in chunks]
    arrays = [block for chunk in chunks for block in chunk]
    _, rows, width = cols.shape
    hidden = arrays[0].shape[1]
    block_rows = width // 2
    anywhere = pl.BlockSpec(memory_space=pl.ANY)
    out_spec = pl.BlockSpec((1, block_rows, hidden), lambda i, ids: (ids[at + i], 0, 0))
    return pl.pallas_call(
        functools.partial(grad_body, layout, first),
        grid_spec=pltpu.PrefetchScalarGridSpec(
            num_scalar_prefetch=1,
            grid=(group,),
            in_specs=[pl.BlockSpec((1, rows, width), lambda i, ids: (ids[at + i], 0, 0))]
            + [pl.BlockSpec(memory_space=pltpu.VMEM)] * len(arrays)
            + ([] if first else [anywhere, anywhere]),
            out_specs=[out_spec, out_spec],
        ),
        out_shape=[out_shape, out_shape],
        input_output_aliases={} if first else {2 + len(arrays): 0, 3 + len(arrays): 1},
        cost_estimate=pl.CostEstimate(
            flops=4 * group * rows * block_rows * hidden,
            bytes_accessed=4 * group * (rows + block_rows) * hidden,
            transcendentals=0,
        ),
        compiler_params=pltpu.CompilerParams(vmem_limit_bytes=12 * 2**20),
        name="grad_stage",
    )(ids, cols, *[in_vmem(array) for array in arrays], *(() if first else totals))


def hot_body(ids_ref, cols_ref, rows_ref, up_in, down_in, up_ref, down_ref):
    del ids_ref
    width = cols_ref.shape[1] // 2
    dims = (((0,), (0,)), ((), ()))
    both = lax.dot_general(cols_ref[...], rows_ref[...], dims, preferred_element_type=F32)
    up_ref[0] = (up_in[0].astype(F32) + both[:width]).astype(BF16)
    down_ref[0] = (down_in[0].astype(F32) + both[width:]).astype(BF16)


def grad_hot(ids, cols, rows, totals):
    hidden = rows.shape[1]
    block_rows = cols.shape[1] // 2
    spec = pl.BlockSpec((1, block_rows, hidden), lambda i, ids: (ids[0], 0, 0))
    out_shape = jax.ShapeDtypeStruct(totals[0].shape, BF16)
    return pl.pallas_call(
        hot_body,
        grid_spec=pltpu.PrefetchScalarGridSpec(
            num_scalar_prefetch=1,
            grid=(1,),
            in_specs=[
                pl.BlockSpec(cols.shape, lambda i, ids: (0, 0)),
                pl.BlockSpec(rows.shape, lambda i, ids: (0, 0)),
                spec,
                spec,
            ],
            out_specs=[spec, spec],
        ),
        out_shape=[out_shape, out_shape],
        input_output_aliases={3: 0, 4: 1},
        compiler_params=pltpu.CompilerParams(vmem_limit_bytes=12 * 2**20),
        name="grad_hot",
    )(ids, cols, rows, *totals)


def ffn_body(
    normal, blocks, x_ref, g_ref, up_hbm, down_hbm, chunk_ref, hot_ref, up_ref, down_ref, pre, sems
):
    width, hidden = up_ref.shape
    rest = x_ref.shape[0] - normal
    rows, units = width // blocks, hidden // blocks
    ups = [pl.ds(k * rows, rows) for k in range(blocks)]
    downs = [pl.ds(k * units, units) for k in range(blocks)]
    copies = [
        pltpu.make_async_copy(up_hbm.at[here], up_ref.at[here], sems.at[0, k])
        for k, here in enumerate(ups)
    ] + [
        pltpu.make_async_copy(down_hbm.at[here], down_ref.at[here], sems.at[1, k])
        for k, here in enumerate(downs)
    ]
    for copy in copies:
        copy.start()
    for k, here in enumerate(ups):
        copies[k].wait()
        term = jnp.dot(x_ref[:, here], up_ref[here, :], preferred_element_type=F32)
        pre[...] = term if k == 0 else pre[...] + term
    for k, here in enumerate(downs):
        value, slope = gelu_pair(pre[:, here])
        value = value.astype(BF16)
        chunk_ref[:normal, here] = value[:normal]
        hot_ref[:rest, here] = value[normal:]
        copies[blocks + k].wait()
        d_act = lax.dot_general(
            g_ref[...], down_ref[here, :], (((1,), (1,)), ((), ())), preferred_element_type=F32
        )
        d_pre = (d_act * slope).astype(BF16)
        chunk_ref[normal:, here] = d_pre[:normal]
        hot_ref[rest:, here] = d_pre[normal:]


def ffn(normal, rows_in, rows_grad, up_local, down_local):
    total = rows_in.shape[0]
    width, hidden = up_local.shape
    blocks = 4
    vmem = pl.BlockSpec(memory_space=pltpu.VMEM)
    hbm = pl.BlockSpec(memory_space=pltpu.HBM)
    return pl.pallas_call(
        functools.partial(ffn_body, normal, blocks),
        in_specs=[vmem, vmem, hbm, hbm],
        out_specs=[vmem] * 4,
        out_shape=[
            jax.ShapeDtypeStruct((2 * normal, hidden), BF16),
            jax.ShapeDtypeStruct((2 * (total - normal), hidden), BF16),
            jax.ShapeDtypeStruct(up_local.shape, BF16),
            jax.ShapeDtypeStruct(down_local.shape, BF16),
        ],
        scratch_shapes=[
            pltpu.VMEM((total, hidden), F32),
            pltpu.SemaphoreType.DMA((2, blocks)),
        ],
        compiler_params=pltpu.CompilerParams(vmem_limit_bytes=12 * 2**20),
        cost_estimate=pl.CostEstimate(
            flops=4 * total * width * hidden,
            bytes_accessed=4 * width * hidden,
            transcendentals=2 * total * hidden,
        ),
        name="ffn",
    )(in_vmem(rows_in), in_vmem(rows_grad), in_hbm(up_local), in_hbm(down_local))


def parts_body(block, chunk_ref, hot_ref, up_ref, down_ref, part_ref, hot_part_ref, act, dpre):
    normal, rest = chunk_ref.shape[0] // 2, hot_ref.shape[0] // 2
    width = up_ref.shape[0]
    act[:normal], act[normal:] = chunk_ref[:normal], hot_ref[:rest]
    dpre[:normal], dpre[normal:] = chunk_ref[normal:], hot_ref[rest:]
    for at in range(0, width, block):
        here = pl.ds(at, block)
        out = jnp.dot(act[...], down_ref[:, here], preferred_element_type=F32).astype(BF16)
        part_ref[:, here], hot_part_ref[:, here] = out[:normal], out[normal:]
        back = lax.dot_general(
            dpre[...], up_ref[here, :], (((1,), (1,)), ((), ())), preferred_element_type=F32
        ).astype(BF16)
        there = pl.ds(width + at, block)
        part_ref[:, there], hot_part_ref[:, there] = back[:normal], back[normal:]


def parts(chunk, hot, up_local, down_local):
    width, hidden = up_local.shape
    normal, rest = chunk.shape[0] // 2, hot.shape[0] // 2
    vmem = pl.BlockSpec(memory_space=pltpu.VMEM)
    return pl.pallas_call(
        functools.partial(parts_body, 256),
        in_specs=[vmem] * 4,
        out_specs=[vmem, vmem],
        out_shape=[
            jax.ShapeDtypeStruct((normal, 2 * width), BF16),
            jax.ShapeDtypeStruct((rest, 2 * width), BF16),
        ],
        scratch_shapes=[pltpu.VMEM((normal + rest, hidden), BF16)] * 2,
        compiler_params=pltpu.CompilerParams(vmem_limit_bytes=12 * 2**20),
        cost_estimate=pl.CostEstimate(
            flops=4 * (normal + rest) * width * hidden,
            bytes_accessed=4 * width * hidden,
            transcendentals=0,
        ),
        name="parts",
    )(in_vmem(chunk), in_vmem(hot), in_vmem(up_local), in_vmem(down_local))


def on_device(tokens, cotangent, gate_probs, expert_ids, route_slots, hot_mask, w_up, w_down):
    count = lax.axis_size("expert")
    planes = lax.axis_size("dp")
    index = lax.axis_index("expert")
    model_width = tokens.shape[1]
    up_local = w_up[0]
    down_local = w_down[0]
    hidden = up_local.shape[1]
    block_rows = model_width // count
    buffers = count * CAP
    swap = flip_bit(count, 1)
    codes = jnp.arange(count, dtype=jnp.int32)
    hot_index = jnp.sum(hot_mask * codes).astype(jnp.int32)
    is_owner = hot_index == index
    sources = ring_sources(count)

    hot_extra = jnp.logical_and(expert_ids == hot_index, route_slots < HCAP)
    place = jnp.where(
        route_slots < CAP,
        expert_ids * CAP + route_slots,
        jnp.where(hot_extra, buffers + route_slots - CAP, -1),
    )
    slot_codes = jnp.arange(buffers + EXTRA, dtype=jnp.int32)
    picks = place[:, :, None] == slot_codes
    pick_first, pick_second = picks[:, 0].astype(BF16), picks[:, 1].astype(BF16)
    pick = pick_first + pick_second
    gate_rows = jnp.sum(jnp.where(picks, gate_probs[:, :, None], 0.0), axis=(0, 1))
    take = (((0,), (0,)), ((), ()))
    rows_x = lax.dot_general(pick, tokens, take, preferred_element_type=F32).astype(BF16)
    rows_g = (
        gate_rows[:, None] * lax.dot_general(pick, cotangent, take, preferred_element_type=F32)
    ).astype(BF16)

    def exchange(value):
        return lax.all_to_all(value, "expert", split_axis=0, concat_axis=0, tiled=True)

    def by_expert(values):
        extra = jnp.broadcast_to(values[None, buffers:], (count, EXTRA, model_width))
        return jnp.concatenate([values[:buffers].reshape(count, CAP, model_width), extra], axis=1)

    rows = jnp.concatenate([by_expert(rows_x), by_expert(rows_g)], axis=2)
    arrived = exchange(rows)
    arrived = jnp.stack(gather_planes(arrived))
    normal = planes * buffers
    flat = arrived[:, :, :CAP].reshape(-1, 2 * model_width)
    hot = arrived[:, :, CAP:].reshape(-1, 2 * model_width)
    flat = jnp.concatenate([flat, jnp.where(is_owner, hot, jnp.zeros_like(hot))])
    chunk, hot_factors, up_held, down_held = ffn(
        normal, flat[:, :model_width], flat[:, model_width:], up_local, down_local
    )
    hot_rows_count = hot_factors.shape[0] // 2

    chunks = ring_gather(chunk)

    def by_column_block(values):
        return values.reshape(-1, count, block_rows)

    both = jnp.concatenate(
        [by_column_block(rows_x[:buffers]), by_column_block(rows_g[:buffers])], axis=2
    )
    columns = exchange(jnp.transpose(both, (1, 0, 2)))
    columns = gather_planes(columns)
    cols = jnp.stack(columns).reshape(planes, count, count, CAP, 2 * block_rows)
    cols = jnp.transpose(cols, (2, 0, 1, 3, 4)).reshape(count, -1, 2 * block_rows)

    part, part_hot = parts(chunk, hot_factors, up_held, down_held)
    part_rows = part.reshape(planes, count, CAP, 2 * model_width)
    part_hot = part_hot.reshape(planes, count, EXTRA, 2 * model_width)
    part_rows = [
        jnp.concatenate([part_rows[s], part_hot[s]], axis=1) for s in range(planes)
    ]
    summed = sum_planes(part_rows)
    pieces = hot_factors.reshape(count, -1, 2 * model_width)
    returned = exchange(jnp.concatenate([summed, pieces], axis=1))
    hot_back = lax.dynamic_index_in_dim(returned[:, CAP:], hot_index, 0, keepdims=False)
    hot_back, piece = hot_back[:EXTRA], hot_back[EXTRA:]
    rows_back = jnp.concatenate(
        [returned[:, :CAP].reshape(buffers, 2 * model_width), hot_back]
    )
    back_out, back_grad = rows_back[:, :model_width], rows_back[:, model_width:]
    layer_out = (
        gate_probs[:, :1] * matmul(pick_first, back_out)
        + gate_probs[:, 1:] * matmul(pick_second, back_out)
    ).astype(BF16)
    grad_tokens = matmul(pick, back_grad).astype(BF16)

    out_shape = jax.ShapeDtypeStruct((count, block_rows, hidden), BF16)
    totals = None
    at = 0
    groups = ring_groups(count)
    for group in groups:
        mine = [chunks[d] for d in group]
        others = [[send(block, swap) for block in chunk] for chunk in mine]
        totals = grad_stage(sources, at, cols, mine + others, totals, out_shape)
        at += 2 * len(group)

    piece = piece.reshape(1, -1, hidden)
    hot_rows = exchange(jnp.broadcast_to(piece, (count,) + piece.shape[1:]))
    hot_rows = hot_rows.reshape(-1, hidden)
    hot_x, hot_g = [
        lax.dynamic_slice_in_dim(hot, half * model_width + index * block_rows, block_rows, 1)
        for half in range(2)
    ]
    none = jnp.zeros((hot_rows_count, block_rows), BF16)
    table = jnp.concatenate(
        [jnp.concatenate([none, hot_g], axis=1), jnp.concatenate([hot_x, none], axis=1)]
    )
    grad_up, grad_down = grad_hot(hot_index[None], table, hot_rows, totals)
    return (layer_out, grad_tokens, grad_up, grad_down)


def solution(mesh):
    placed = (
        P(("dp", "expert"), None),
        P(("dp", "expert"), None),
        P(("dp", "expert"), None),
        P(("dp", "expert"), None),
        P(("dp", "expert"), None),
        P(),
        P("expert", None, "dp"),
        P("expert", "dp", None),
    )

    return jax.shard_map(
        on_device,
        mesh=mesh,
        in_specs=placed,
        out_specs=(
            P(("dp", "expert"), None),
            P(("dp", "expert"), None),
            P(None, "expert", "dp"),
            P(None, "expert", "dp"),
        ),
        check_vma=False,
    )
```

profile of v0, /device:TPU:11, one launch (start us, length us, event | category | flops | bytes accessed | tf_op | source)
XLA Modules:
  0.0 190.6 jit_solution(8669134159987470562)
XLA Ops:
  7.1 19.9 %all_to_all.20 = bf16[16,4,4096]{2,1,0:T(4,128)(2,1)S(1)} all-to-all(bf16[16,4,4096]{2,1,0:T(4,128)(2,1)S(1)} %maximum_maximum_fusion), channel_id=1, replica_groups=mesh['dp'=2,'expert'=16] {'expert'}, dimensions={0} | all-to-all | bytes 1048576 | tf_op jit(solution)/shard_map/all_to_all | solution.py:350
  28.9 11.5 %collective-permute-done = bf16[16,4,4096]{2,1,0:T(4,128)(2,1)S(1)} collective-permute-done((bf16[16,4,4096]{2,1,0:T(4,128)(2,1)S(1)}, bf16[16,4,4096]{2,1,0:T(4,128)(2,1)S(1)}, u32[]{:S(2)}, u32[]{:S(2)}) %collective-permute-start) | collective-permute-done | bytes 524320 | tf_op jit(solution)/shard_map/ppermute | solution.py:58
  42.5 7.8 %ffn.1 = (bf16[128,2048]{1,0:T(8,128)(2,1)S(1)}, bf16[128,2048]{1,0:T(8,128)(2,1)S(1)}, bf16[2048,2048]{1,0:T(8,128)(2,1)S(1)}, bf16[2048,2048]{1,0:T(8,128)(2,1)S(1)}) custom-call(bf16[128,2048]{1,0:T(8,128)(2,1)S(1)} %get-tuple-element.41.x_ref, bf16[128,2048]{1,0:T(8,128)(2,1)S(1)} %get-tuple-element.40.g_ref, bf16[2048,2048]{1,0:T(8,128)(2,1)} %bitcast.49, ...), custom_call_target="tpu_custom_call" | custom-call | flops 2147483648 | bytes 16777216 | tf_op jit(solution)/shard_map/ffn/pallas_call | solution.py:253
  51.8 3.9 %parts.1 = (bf16[64,4096]{1,0:T(8,128)(2,1)S(1)}, bf16[64,4096]{1,0:T(8,128)(2,1)S(1)}) custom-call(bf16[128,2048]{1,0:T(8,128)(2,1)S(1)} %get-tuple-element.22.chunk_ref.refs_0_, bf16[128,2048]{1,0:T(8,128)(2,1)S(1)} %get-tuple-element.23.hot_ref, bf16[2048,2048]{1,0:T(8,128)(2,1)S(1)} %get-tuple-element.24.up_ref, ...), custom_call_target="tpu_custom_call" | custom-call | flops 2147483648 | bytes 16777216 | tf_op jit(solution)/shard_map/parts/pallas_call | solution.py:297
  62.3 6.6 %all-to-all-start.3 = ((bf16[16,32,256]{2,1,0:T(8,128)(2,1)}), bf16[16,32,256]{2,1,0:T(8,128)(2,1)S(1)}, u32[]{:S(2)}, u32[]{:S(2)}) async-start(bf16[16,32,256]{2,1,0:T(8,128)(2,1)} %maximum_bitcast_fusion.1), calls=%async_computation.3 | async-start | bytes 524288 | tf_op jit(solution)/shard_map/all_to_all | solution.py:350
  69.2 1.8 squeeze.30
  71.1 1.8 squeeze.31
  74.4 1.9 add_convert_fusion
  77.8 6.6 %all-to-all-start.1 = ((bf16[16,8,4096]{2,1,0:T(8,128)(2,1)}), bf16[16,8,4096]{2,1,0:T(8,128)(2,1)}, u32[]{:S(2)}, u32[]{:S(2)}) async-start(bf16[16,8,4096]{2,1,0:T(8,128)(2,1)} %pad_maximum_fusion), calls=%async_computation.1 | async-start | bytes 2097152 | tf_op jit(solution)/shard_map/all_to_all | solution.py:350
  84.3 1.8 collective-permute-done.8.refs_1_
  86.1 2.3 %collective-permute-start.9 = (bf16[128,2048]{1,0:T(8,128)(2,1)S(1)}, bf16[128,2048]{1,0:T(8,128)(2,1)S(1)}, u32[]{:S(2)}, u32[]{:S(2)}) collective-permute-start(bf16[128,2048]{1,0:T(8,128)(2,1)S(1)} %collective-permute-done.8.refs_1_), channel_id=1, source_target_pairs={{0,2},{1,3},{4,0},{5,1},{8,4},{9,5},{12,8},{13,9},{14,12},{15,13},... | collective-permute-start | bytes 1572872 | tf_op jit(solution)/shard_map/ppermute | solution.py:53
  88.5 4.5 %collective-permute-start.19 = (bf16[128,2048]{1,0:T(8,128)(2,1)S(1)}, bf16[128,2048]{1,0:T(8,128)(2,1)}, u32[]{:S(2)}, u32[]{:S(2)}) collective-permute-start(bf16[128,2048]{1,0:T(8,128)(2,1)S(1)} %get-tuple-element.22.chunk_ref.refs_0_), channel_id=1, source_target_pairs={{0,1},{1,0},{2,3},{3,2},{4,5},{5,4},{6,7},{7,6},{8,9},{9,8},{10,11... | collective-permute-start | bytes 1572872 | tf_op jit(solution)/shard_map/ppermute | solution.py:53
  93.5 26.4 %collective-permute-done.9.refs_1_ = bf16[128,2048]{1,0:T(8,128)(2,1)S(1)} collective-permute-done((bf16[128,2048]{1,0:T(8,128)(2,1)S(1)}, bf16[128,2048]{1,0:T(8,128)(2,1)S(1)}, u32[]{:S(2)}, u32[]{:S(2)}) %collective-permute-start.9) | collective-permute-done | bytes 524320 | tf_op jit(solution)/shard_map/ppermute | solution.py:53
  123.1 5.4 %collective-permute-done.2 = bf16[16,32,256]{2,0,1:T(8,128)(2,1)S(1)} collective-permute-done((bf16[16,32,256]{2,0,1:T(8,128)(2,1)}, bf16[16,32,256]{2,0,1:T(8,128)(2,1)S(1)}, u32[]{:S(2)}, u32[]{:S(2)}) %collective-permute-start.2) | collective-permute-done | bytes 262176 | tf_op jit(solution)/shard_map/ppermute | solution.py:58
  128.6 1.8 collective-permute-start.15
  130.4 2.2 %collective-permute-start.10 = (bf16[64,2048]{1,0:T(8,128)(2,1)}, bf16[64,2048]{1,0:T(8,128)(2,1)S(1)}, u32[]{:S(2)}, u32[]{:S(2)}) collective-permute-start(bf16[64,2048]{1,0:T(8,128)(2,1)} %slice.122), channel_id=1, source_target_pairs={{0,2},{1,3},{4,0},{5,1},{8,4},{9,5},{12,8},{13,9},{14,12},{15,13},... | collective-permute-start | bytes 786440 | tf_op jit(solution)/shard_map/ppermute | solution.py:53
  142.4 3.6 %grad_stage.5 = (bf16[16,128,2048]{2,1,0:T(8,128)(2,1)}, bf16[16,128,2048]{2,1,0:T(8,128)(2,1)}) custom-call(s32[16]{0:T(128)S(1)} %fusion.17.ids_ref, bf16[16,64,256]{2,1,0:T(8,128)(2,1)S(1)} %reshape.72.cols_ref, bf16[128,2048]{1,0:T(8,128)(2,1)S(1)} %get-tuple-element.22.chunk_ref.refs_0_, bf16[128,2048]{1,0:T(8,128)(2,1)} %collective-permute-done.19.refs_1_), custom_call_target="tpu_custom_call" | custom-call | flops 134217728 | bytes 3145728 | tf_op jit(solution)/shard_map/grad_stage/pallas_call | solution.py:156
  145.9 5.1 %grad_stage.6 = (bf16[16,128,2048]{2,1,0:T(8,128)(2,1)}, bf16[16,128,2048]{2,1,0:T(8,128)(2,1)}) custom-call(s32[16]{0:T(128)S(1)} %fusion.17.ids_ref, bf16[16,64,256]{2,1,0:T(8,128)(2,1)S(1)} %reshape.72.cols_ref, bf16[128,2048]{1,0:T(8,128)(2,1)S(1)} %collective-permute-done.3.refs_0_, ...), custom_call_target="tpu_custom_call", output_to_operand_aliasing={{0}: (6, {}), {1}: (7, {})} | custom-call | flops 268435456 | bytes 6291456 | tf_op jit(solution)/shard_map/grad_stage/pallas_call | solution.py:156
  151.1 5.3 %grad_stage.7 = (bf16[16,128,2048]{2,1,0:T(8,128)(2,1)}, bf16[16,128,2048]{2,1,0:T(8,128)(2,1)}) custom-call(s32[16]{0:T(128)S(1)} %fusion.17.ids_ref, bf16[16,64,256]{2,1,0:T(8,128)(2,1)S(1)} %reshape.72.cols_ref, bf16[128,2048]{1,0:T(8,128)(2,1)} %collective-permute-done.4.refs_0_, ...), custom_call_target="tpu_custom_call", output_to_operand_aliasing={{0}: (6, {}), {1}: (7, {})} | custom-call | flops 268435456 | bytes 6291456 | tf_op jit(solution)/shard_map/grad_stage/pallas_call | solution.py:156
  156.4 5.2 %grad_stage.8 = (bf16[16,128,2048]{2,1,0:T(8,128)(2,1)}, bf16[16,128,2048]{2,1,0:T(8,128)(2,1)}) custom-call(s32[16]{0:T(128)S(1)} %fusion.17.ids_ref, bf16[16,64,256]{2,1,0:T(8,128)(2,1)S(1)} %reshape.72.cols_ref, bf16[128,2048]{1,0:T(8,128)(2,1)S(1)} %collective-permute-done.5.refs_0_, ...), custom_call_target="tpu_custom_call", output_to_operand_aliasing={{0}: (6, {}), {1}: (7, {})} | custom-call | flops 268435456 | bytes 6291456 | tf_op jit(solution)/shard_map/grad_stage/pallas_call | solution.py:156
  161.6 3.5 %grad_stage.9 = (bf16[16,128,2048]{2,1,0:T(8,128)(2,1)}, bf16[16,128,2048]{2,1,0:T(8,128)(2,1)}) custom-call(s32[16]{0:T(128)S(1)} %fusion.17.ids_ref, bf16[16,64,256]{2,1,0:T(8,128)(2,1)S(1)} %reshape.72.cols_ref, bf16[64,2048]{1,0:T(8,128)(2,1)} %collective-permute-done.6.refs_0_, ...), custom_call_target="tpu_custom_call", output_to_operand_aliasing={{0}: (6, {}), {1}: (7, {})} | custom-call | flops 134217728 | bytes 3145728 | tf_op jit(solution)/shard_map/grad_stage/pallas_call | solution.py:156
  169.0 4.7 %all-to-all-start.2 = ((bf16[16,8,2048]{2,1,0:T(8,128)(2,1)}), bf16[16,8,2048]{2,1,0:T(8,128)(2,1)S(1)}, u32[]{:S(2)}, u32[]{:S(2)}) async-start(bf16[16,8,2048]{2,1,0:T(8,128)(2,1)} %broadcast_in_dim.62), calls=%async_computation.2 | async-start | bytes 1048576 | tf_op jit(solution)/shard_map/all_to_all | solution.py:350
  176.3 10.9 %all-to-all-done.2 = bf16[16,8,2048]{2,1,0:T(8,128)(2,1)S(1)} async-done(((bf16[16,8,2048]{2,1,0:T(8,128)(2,1)}), bf16[16,8,2048]{2,1,0:T(8,128)(2,1)S(1)}, u32[]{:S(2)}, u32[]{:S(2)}) %all-to-all-start.2) | async-done | bytes 524320 | tf_op jit(solution)/shard_map/all_to_all | solution.py:350
  187.3 3.3 %grad_hot.1 = (bf16[16,128,2048]{2,1,0:T(8,128)(2,1)}, bf16[16,128,2048]{2,1,0:T(8,128)(2,1)}) custom-call(s32[1]{0:T(128)} %bitcast.9.ids_ref, bf16[128,256]{1,0:T(8,128)(2,1)S(1)} %fusion.9.cols_ref, bf16[128,2048]{1,0:T(8,128)(2,1)S(1)} %bitcast.48, bf16[16,128,2048]{2,1,0:T(8,128)(2,1)} %get-tuple-element.36.up_in, ...), custom_call_target="tpu_custom_call", output_to_operand_aliasing={{0}: (3, {}), {1}: (4, {})} | custom-call | tf_op jit(solution)/shard_map/grad_hot/pallas_call | solution.py:192
  (96 shorter events, 39.1 us)
Async XLA Ops:
  27.0 13.4 %collective-permute-start = (bf16[16,4,4096]{2,1,0:T(4,128)(2,1)S(1)}, bf16[16,4,4096]{2,1,0:T(4,128)(2,1)S(1)}, u32[]{:S(2)}, u32[]{:S(2)}) collective-permute-start(bf16[16,4,4096]{2,1,0:T(4,128)(2,1)S(1)} %all_to_all.20), channel_id=1, source_target_pairs={{0,16},{16,0},{1,17},{17,1},{2,18},{18,2},{3,19},{19,3},{4,20},{20... | collective-permute-start | bytes 1572872 | tf_op jit(solution)/shard_map/ppermute | solution.py:58
  50.3 22.6 %collective-permute-start.7 = (bf16[128,2048]{1,0:T(8,128)(2,1)S(1)}, bf16[128,2048]{1,0:T(8,128)(2,1)S(1)}, u32[]{:S(2)}, u32[]{:S(2)}) collective-permute-start(bf16[128,2048]{1,0:T(8,128)(2,1)S(1)} %get-tuple-element.22.chunk_ref.refs_0_), channel_id=1, source_target_pairs={{0,2},{1,3},{4,0},{5,1},{8,4},{9,5},{12,8},{13,9},{14,12},{15,13},... | collective-permute-start | bytes 1572872 | tf_op jit(solution)/shard_map/ppermute | solution.py:53
  50.4 23.7 %collective-permute-start.3 = (bf16[128,2048]{1,0:T(8,128)(2,1)S(1)}, bf16[128,2048]{1,0:T(8,128)(2,1)S(1)}, u32[]{:S(2)}, u32[]{:S(2)}) collective-permute-start(bf16[128,2048]{1,0:T(8,128)(2,1)S(1)} %get-tuple-element.22.chunk_ref.refs_0_), channel_id=1, source_target_pairs={{0,4},{1,5},{4,8},{5,9},{8,12},{9,13},{12,14},{13,15},{14,10},{15,... | collective-permute-start | bytes 1572872 | tf_op jit(solution)/shard_map/ppermute | solution.py:53
  55.8 65.9 %copy-start.6 = (f32[128,2]{0,1:T(2,128)S(1)}, f32[128,2]{0,1:T(2,128)}, u32[]{:S(2)}) copy-start(f32[128,2]{0,1:T(2,128)} %param.12) | copy-start | bytes 3076
  59.4 15.0 %collective-permute-start.1 = (bf16[16,4,4096]{2,1,0:T(4,128)(2,1)}, bf16[16,4,4096]{2,1,0:T(4,128)(2,1)}, u32[]{:S(2)}, u32[]{:S(2)}) collective-permute-start(bf16[16,4,4096]{2,1,0:T(4,128)(2,1)} %pad_maximum_fusion.3), channel_id=1, source_target_pairs={{0,16},{16,0},{1,17},{17,1},{2,18},{18,2},{3,19},{19,3},{4,20},{20... | collective-permute-start | bytes 1572872 | tf_op jit(solution)/shard_map/ppermute | solution.py:58
  62.3 15.5 %all-to-all-start.3 = ((bf16[16,32,256]{2,1,0:T(8,128)(2,1)}), bf16[16,32,256]{2,1,0:T(8,128)(2,1)S(1)}, u32[]{:S(2)}, u32[]{:S(2)}) async-start(bf16[16,32,256]{2,1,0:T(8,128)(2,1)} %maximum_bitcast_fusion.1), calls=%async_computation.3 | async-start | bytes 524288 | tf_op jit(solution)/shard_map/all_to_all | solution.py:350
  72.9 13.2 %collective-permute-start.8 = (bf16[128,2048]{1,0:T(8,128)(2,1)S(1)}, bf16[128,2048]{1,0:T(8,128)(2,1)S(1)}, u32[]{:S(2)}, u32[]{:S(2)}) collective-permute-start(bf16[128,2048]{1,0:T(8,128)(2,1)S(1)} %collective-permute-done.7.refs_1_), channel_id=1, source_target_pairs={{0,2},{1,3},{4,0},{5,1},{8,4},{9,5},{12,8},{13,9},{14,12},{15,13},... | collective-permute-start | bytes 1572872 | tf_op jit(solution)/shard_map/ppermute | solution.py:53
  74.1 14.3 %collective-permute-start.4 = (bf16[128,2048]{1,0:T(8,128)(2,1)S(1)}, bf16[128,2048]{1,0:T(8,128)(2,1)}, u32[]{:S(2)}, u32[]{:S(2)}) collective-permute-start(bf16[128,2048]{1,0:T(8,128)(2,1)S(1)} %collective-permute-done.3.refs_0_), channel_id=1, source_target_pairs={{0,4},{1,5},{4,8},{5,9},{8,12},{9,13},{12,14},{13,15},{14,10},{15,... | collective-permute-start | bytes 1572872 | tf_op jit(solution)/shard_map/ppermute | solution.py:53
  77.8 87.3 %all-to-all-start.1 = ((bf16[16,8,4096]{2,1,0:T(8,128)(2,1)}), bf16[16,8,4096]{2,1,0:T(8,128)(2,1)}, u32[]{:S(2)}, u32[]{:S(2)}) async-start(bf16[16,8,4096]{2,1,0:T(8,128)(2,1)} %pad_maximum_fusion), calls=%async_computation.1 | async-start | bytes 2097152 | tf_op jit(solution)/shard_map/all_to_all | solution.py:350
  86.1 33.8 %collective-permute-start.9 = (bf16[128,2048]{1,0:T(8,128)(2,1)S(1)}, bf16[128,2048]{1,0:T(8,128)(2,1)S(1)}, u32[]{:S(2)}, u32[]{:S(2)}) collective-permute-start(bf16[128,2048]{1,0:T(8,128)(2,1)S(1)} %collective-permute-done.8.refs_1_), channel_id=1, source_target_pairs={{0,2},{1,3},{4,0},{5,1},{8,4},{9,5},{12,8},{13,9},{14,12},{15,13},... | collective-permute-start | bytes 1572872 | tf_op jit(solution)/shard_map/ppermute | solution.py:53
  88.4 33.0 %collective-permute-start.5 = (bf16[128,2048]{1,0:T(8,128)(2,1)}, bf16[128,2048]{1,0:T(8,128)(2,1)S(1)}, u32[]{:S(2)}, u32[]{:S(2)}) collective-permute-start(bf16[128,2048]{1,0:T(8,128)(2,1)} %collective-permute-done.4.refs_0_), channel_id=1, source_target_pairs={{0,4},{1,5},{4,8},{5,9},{8,12},{9,13},{12,14},{13,15},{14,10},{15,... | collective-permute-start | bytes 1572872 | tf_op jit(solution)/shard_map/ppermute | solution.py:53
  88.5 41.9 %collective-permute-start.19 = (bf16[128,2048]{1,0:T(8,128)(2,1)S(1)}, bf16[128,2048]{1,0:T(8,128)(2,1)}, u32[]{:S(2)}, u32[]{:S(2)}) collective-permute-start(bf16[128,2048]{1,0:T(8,128)(2,1)S(1)} %get-tuple-element.22.chunk_ref.refs_0_), channel_id=1, source_target_pairs={{0,1},{1,0},{2,3},{3,2},{4,5},{5,4},{6,7},{7,6},{8,9},{9,8},{10,11... | collective-permute-start | bytes 1572872 | tf_op jit(solution)/shard_map/ppermute | solution.py:53
  93.0 39.6 %collective-permute-start.18 = (bf16[128,2048]{1,0:T(8,128)(2,1)S(1)}, bf16[128,2048]{1,0:T(8,128)(2,1)}, u32[]{:S(2)}, u32[]{:S(2)}) collective-permute-start(bf16[128,2048]{1,0:T(8,128)(2,1)S(1)} %collective-permute-done.7.refs_1_), channel_id=1, source_target_pairs={{0,1},{1,0},{2,3},{3,2},{4,5},{5,4},{6,7},{7,6},{8,9},{9,8},{10,11... | collective-permute-start | bytes 1572872 | tf_op jit(solution)/shard_map/ppermute | solution.py:53
  93.0 39.6 %collective-permute-start.17 = (bf16[128,2048]{1,0:T(8,128)(2,1)S(1)}, bf16[128,2048]{1,0:T(8,128)(2,1)}, u32[]{:S(2)}, u32[]{:S(2)}) collective-permute-start(bf16[128,2048]{1,0:T(8,128)(2,1)S(1)} %collective-permute-done.3.refs_0_), channel_id=1, source_target_pairs={{0,1},{1,0},{2,3},{3,2},{4,5},{5,4},{6,7},{7,6},{8,9},{9,8},{10,11... | collective-permute-start | bytes 1572872 | tf_op jit(solution)/shard_map/ppermute | solution.py:53
  119.9 13.7 %collective-permute-start.16 = (bf16[128,2048]{1,0:T(8,128)(2,1)S(1)}, bf16[128,2048]{1,0:T(8,128)(2,1)}, u32[]{:S(2)}, u32[]{:S(2)}) collective-permute-start(bf16[128,2048]{1,0:T(8,128)(2,1)S(1)} %collective-permute-done.8.refs_1_), channel_id=1, source_target_pairs={{0,1},{1,0},{2,3},{3,2},{4,5},{5,4},{6,7},{7,6},{8,9},{9,8},{10,11... | collective-permute-start | bytes 1572872 | tf_op jit(solution)/shard_map/ppermute | solution.py:53
  121.5 7.1 %collective-permute-start.2 = (bf16[16,32,256]{2,0,1:T(8,128)(2,1)}, bf16[16,32,256]{2,0,1:T(8,128)(2,1)S(1)}, u32[]{:S(2)}, u32[]{:S(2)}) collective-permute-start(bf16[16,32,256]{2,0,1:T(8,128)(2,1)} %copy.30), channel_id=1, source_target_pairs={{0,16},{16,0},{1,17},{17,1},{2,18},{18,2},{3,19},{19,3},{4,20},{20... | collective-permute-start | bytes 786440 | tf_op jit(solution)/shard_map/ppermute | solution.py:58
  128.6 22.5 %collective-permute-start.15 = (bf16[128,2048]{1,0:T(8,128)(2,1)}, bf16[128,2048]{1,0:T(8,128)(2,1)}, u32[]{:S(2)}, u32[]{:S(2)}) collective-permute-start(bf16[128,2048]{1,0:T(8,128)(2,1)} %collective-permute-done.4.refs_0_), channel_id=1, source_target_pairs={{0,1},{1,0},{2,3},{3,2},{4,5},{5,4},{6,7},{7,6},{8,9},{9,8},{10,11... | collective-permute-start | bytes 1572872 | tf_op jit(solution)/shard_map/ppermute | solution.py:53
  130.4 9.7 %collective-permute-start.10 = (bf16[64,2048]{1,0:T(8,128)(2,1)}, bf16[64,2048]{1,0:T(8,128)(2,1)S(1)}, u32[]{:S(2)}, u32[]{:S(2)}) collective-permute-start(bf16[64,2048]{1,0:T(8,128)(2,1)} %slice.122), channel_id=1, source_target_pairs={{0,2},{1,3},{4,0},{5,1},{8,4},{9,5},{12,8},{13,9},{14,12},{15,13},... | collective-permute-start | bytes 786440 | tf_op jit(solution)/shard_map/ppermute | solution.py:53
  132.6 8.0 %collective-permute-start.6 = (bf16[64,2048]{1,0:T(8,128)(2,1)}, bf16[64,2048]{1,0:T(8,128)(2,1)}, u32[]{:S(2)}, u32[]{:S(2)}) collective-permute-start(bf16[64,2048]{1,0:T(8,128)(2,1)} %slice.121), channel_id=1, source_target_pairs={{0,4},{1,5},{4,8},{5,9},{8,12},{9,13},{12,14},{13,15},{14,10},{15,... | collective-permute-start | bytes 786440 | tf_op jit(solution)/shard_map/ppermute | solution.py:53
  132.6 23.8 %collective-permute-start.14 = (bf16[128,2048]{1,0:T(8,128)(2,1)S(1)}, bf16[128,2048]{1,0:T(8,128)(2,1)}, u32[]{:S(2)}, u32[]{:S(2)}) collective-permute-start(bf16[128,2048]{1,0:T(8,128)(2,1)S(1)} %collective-permute-done.9.refs_1_), channel_id=1, source_target_pairs={{0,1},{1,0},{2,3},{3,2},{4,5},{5,4},{6,7},{7,6},{8,9},{9,8},{10,11... | collective-permute-start | bytes 1572872 | tf_op jit(solution)/shard_map/ppermute | solution.py:53
  133.7 22.8 %collective-permute-start.13 = (bf16[128,2048]{1,0:T(8,128)(2,1)S(1)}, bf16[128,2048]{1,0:T(8,128)(2,1)}, u32[]{:S(2)}, u32[]{:S(2)}) collective-permute-start(bf16[128,2048]{1,0:T(8,128)(2,1)S(1)} %collective-permute-done.5.refs_0_), channel_id=1, source_target_pairs={{0,1},{1,0},{2,3},{3,2},{4,5},{5,4},{6,7},{7,6},{8,9},{9,8},{10,11... | collective-permute-start | bytes 1572872 | tf_op jit(solution)/shard_map/ppermute | solution.py:53
  140.1 21.5 %collective-permute-start.12 = (bf16[64,2048]{1,0:T(8,128)(2,1)S(1)}, bf16[64,2048]{1,0:T(8,128)(2,1)S(1)}, u32[]{:S(2)}, u32[]{:S(2)}) collective-permute-start(bf16[64,2048]{1,0:T(8,128)(2,1)S(1)} %collective-permute-done.10.refs_1_), channel_id=1, source_target_pairs={{0,1},{1,0},{2,3},{3,2},{4,5},{5,4},{6,7},{7,6},{8,9},{9,8},{10,11... | collective-permute-start | bytes 786440 | tf_op jit(solution)/shard_map/ppermute | solution.py:53
  140.6 21.0 %collective-permute-start.11 = (bf16[64,2048]{1,0:T(8,128)(2,1)}, bf16[64,2048]{1,0:T(8,128)(2,1)S(1)}, u32[]{:S(2)}, u32[]{:S(2)}) collective-permute-start(bf16[64,2048]{1,0:T(8,128)(2,1)} %collective-permute-done.6.refs_0_), channel_id=1, source_target_pairs={{0,1},{1,0},{2,3},{3,2},{4,5},{5,4},{6,7},{7,6},{8,9},{9,8},{10,11... | collective-permute-start | bytes 786440 | tf_op jit(solution)/shard_map/ppermute | solution.py:53
  169.0 18.3 %all-to-all-start.2 = ((bf16[16,8,2048]{2,1,0:T(8,128)(2,1)}), bf16[16,8,2048]{2,1,0:T(8,128)(2,1)S(1)}, u32[]{:S(2)}, u32[]{:S(2)}) async-start(bf16[16,8,2048]{2,1,0:T(8,128)(2,1)} %broadcast_in_dim.62), calls=%async_computation.2 | async-start | bytes 1048576 | tf_op jit(solution)/shard_map/all_to_all | solution.py:350
  (6 other events, 66.1 us)
where the time goes:
time: 193 us; the launch traced here: 191 us
  waiting for transfers between devices  56 us (29%)
  starting transfers between devices  38.3 us (20%)
  Pallas kernels  37.7 us (20%)
  blocking collectives  19.9 us (10%)
  local copies, waits for them, and re-layouts  18.5 us (10%)
  other arithmetic  12.5 us (6%)
  matrix products  4.08 us (2%)
  between operations  3.64 us (2%)
    ppermute x17, waiting for transfers between devices, send(): return lax.ppermute(value, 'expert', pairs)  28.2 us
    pallas_call x5, Pallas kernels, grad_stage(): pl.pallas_call(functools.partial(grad_body, layout, first), grid_spec=plt...  22.6 us
    all_to_all x1, blocking collectives, exchange(): lax.all_to_all(value, 'expert', split_axis=0, concat_axis=0, tiled=True)  19.9 us
    all_to_all x3, starting transfers between devices, exchange(): lax.all_to_all(value, 'expert', split_axis=0, concat_axis=0, tiled=True)  17.8 us
    ppermute x17, starting transfers between devices, send(): return lax.ppermute(value, 'expert', pairs)  17.7 us
    ppermute x3, waiting for transfers between devices, dp_shift(): lax.ppermute(value, 'dp', [(p, (p + shift) % count) for p in range(count)])  16.9 us
    all_to_all x3, waiting for transfers between devices, exchange(): lax.all_to_all(value, 'expert', split_axis=0, concat_axis=0, tiled=True)  10.9 us
    pallas_call x1, Pallas kernels, ffn(): pl.pallas_call(functools.partial(ffn_body, normal, blocks), in_specs=[vme...  7.8 us
  transfers between devices with their start and end apart: 23, of which 5 were waited for; matrix products, arithmetic and copies ran while one was open for 12% of the time, Pallas kernels for 14%

commit v1 on v0

v1 whole, which is shorter than its diff:
```python
import functools

import jax
import jax.numpy as jnp
from jax import lax
from jax.experimental import pallas as pl
from jax.experimental.pallas import tpu as pltpu
from jax.sharding import PartitionSpec as P


CAP = 2
HCAP = 4
EXTRA = HCAP - CAP
BF16 = jnp.bfloat16
F32 = jnp.float32


def in_vmem(value):
    return pltpu.with_memory_space_constraint(value, pltpu.VMEM)


def in_hbm(value):
    return pltpu.with_memory_space_constraint(value, pltpu.HBM)


def gelu_pair(preact):
    normal_cdf = 0.5 * (1.0 + lax.erf(preact * 0.7071067811865476))
    density = jnp.exp(-0.5 * preact * preact) * 0.3989422804014327
    return (preact * normal_cdf, normal_cdf + preact * density)


def matmul(left, right):
    return jnp.dot(left, right, preferred_element_type=F32)


def chip_ring(device_count):
    chips = device_count // 2
    half = chips // 2
    return [2 * i for i in range(half)] + [2 * i + 1 for i in reversed(range(chips - half))]


def ring_pairs(device_count, shift):
    ring = chip_ring(device_count)
    size = len(ring)
    return [
        (2 * ring[k] + core, 2 * ring[(k + shift) % size] + core)
        for k in range(size)
        for core in range(2)
    ]


def send(value, pairs):
    return lax.ppermute(value, "expert", pairs)


def dp_shift(value, shift):
    count = lax.axis_size("dp")
    return lax.ppermute(value, "dp", [(p, (p + shift) % count) for p in range(count)])


def gather_planes(own):
    count = lax.axis_size("dp")
    return [own] + [dp_shift(own, -shift) for shift in range(1, count)]


def flip_bit(device_count, bit):
    return [(i, i ^ bit) for i in range(device_count)]


def ring_gather(value, split_far=True):
    count = lax.axis_size("expert")
    size = count // 2
    right, left = ring_pairs(count, 1), ring_pairs(count, -1)
    got = {0: [value]}
    going_right = going_left = value
    for step in range(1, (size - 1) // 2 + 1):
        going_right = send(going_right, right)
        going_left = send(going_left, left)
        got[-step], got[step] = [going_right], [going_left]
    if size % 2 == 0 and not split_far:
        got[-(size // 2)] = [send(going_right, right)]
    elif size % 2 == 0:
        half = value.shape[0] // 2
        far_right = send(going_right[:half], right)
        far_left = send(going_left[half:], left)
        got[-(size // 2)] = [far_right, far_left]
    return got


def ring_groups(count):
    size = count // 2
    groups = [[0]] + [[-step, step] for step in range(1, (size - 1) // 2 + 1)]
    return groups + ([[-(size // 2)]] if size % 2 == 0 else [])


def ring_sources(count):
    size = count // 2
    half = size // 2
    index = lax.axis_index("expert")
    chip, core = index // 2, index % 2
    place = jnp.where(chip % 2 == 0, chip // 2, size - 1 - chip // 2)
    groups = ring_groups(count)
    distances = jnp.array([d for group in groups for d in group * 2], dtype=jnp.int32)
    other = jnp.array(
        [o for group in groups for o in [0] * len(group) + [1] * len(group)], dtype=jnp.int32
    )
    there = lax.rem(place + distances + size, size)
    chip_there = jnp.where(there < half, 2 * there, 2 * (size - 1 - there) + 1)
    return 2 * chip_there + jnp.where(other == 1, 1 - core, core)


def grad_body(layout, first, ids_ref, cols_ref, *refs):
    del ids_ref
    blocks = sum(layout)
    up_ref, down_ref = refs[blocks + (0 if first else 2) :]
    width = cols_ref.shape[2] // 2
    rows = cols_ref.shape[1]
    dims = (((0,), (0,)), ((), ()))
    step = pl.program_id(0)
    at = 0
    for k, parts in enumerate(layout):
        if parts == 1:
            act, dpre = refs[at].at[:rows], refs[at].at[rows:]
        else:
            act, dpre = refs[at], refs[at + 1]
        at += parts

        @pl.when(step == k)
        def _(act=act, dpre=dpre):
            up = lax.dot_general(
                cols_ref[0, :, :width], dpre[...], dims, preferred_element_type=F32
            )
            up_ref[0] = up.astype(BF16)
            down = lax.dot_general(
                cols_ref[0, :, width:], act[...], dims, preferred_element_type=F32
            )
            down_ref[0] = down.astype(BF16)


def grad_stage(ids, at, cols, chunks, totals, out_shape):
    group = len(chunks)
    first = totals is None
    layout = [len(chunk) for chunk in chunks]
    arrays = [block for chunk in chunks for block in chunk]
    _, rows, width = cols.shape
    hidden = arrays[0].shape[1]
    block_rows = width // 2
    anywhere = pl.BlockSpec(memory_space=pl.ANY)
    out_spec = pl.BlockSpec((1, block_rows, hidden), lambda i, ids: (ids[at + i], 0, 0))
    return pl.pallas_call(
        functools.partial(grad_body, layout, first),
        grid_spec=pltpu.PrefetchScalarGridSpec(
            num_scalar_prefetch=1,
            grid=(group,),
            in_specs=[pl.BlockSpec((1, rows, width), lambda i, ids: (ids[at + i], 0, 0))]
            + [pl.BlockSpec(memory_space=pltpu.VMEM)] * len(arrays)
            + ([] if first else [anywhere, anywhere]),
            out_specs=[out_spec, out_spec],
        ),
        out_shape=[out_shape, out_shape],
        input_output_aliases={} if first else {2 + len(arrays): 0, 3 + len(arrays): 1},
        cost_estimate=pl.CostEstimate(
            flops=4 * group * rows * block_rows * hidden,
            bytes_accessed=4 * group * (rows + block_rows) * hidden,
            transcendentals=0,
        ),
        compiler_params=pltpu.CompilerParams(vmem_limit_bytes=12 * 2**20),
        name="grad_stage",
    )(ids, cols, *[in_vmem(array) for array in arrays], *(() if first else totals))


def last_body(
    group, at, ids_ref, cols_ref, table_ref, rows_ref, *refs
):
    acts, dpres = refs[0 : 2 * group : 2], refs[1 : 2 * group : 2]
    up_in, down_in, up_out, down_out = refs[2 * group : 2 * group + 4]
    held, both, sems = refs[2 * group + 4 :]
    del up_in, down_in
    hot = ids_ref[ids_ref.shape[0] - 1]
    block_rows = held.shape[2]
    dims = (((0,), (0,)), ((), ()))
    outs = (up_out, down_out)
    ours = [ids_ref[at + k] for k in range(group)]
    elsewhere = functools.reduce(jnp.logical_and, [expert != hot for expert in ours])

    def moves(slot, expert, into):
        pairs = [(held.at[slot, side], outs[side].at[expert]) for side in range(2)]
        pairs = [(b, a) for a, b in pairs] if into else pairs
        return [
            pltpu.make_async_copy(a, b, sems.at[slot, side]) for side, (a, b) in enumerate(pairs)
        ]

    @pl.when(elsewhere)
    def _():
        for copy in moves(group, hot, True):
            copy.start()

    both[...] = lax.dot_general(
        table_ref[...], rows_ref[...], dims, preferred_element_type=F32
    )
    for k in range(group):
        cols = cols_ref[ours[k]]
        mine = jnp.where(ours[k] == hot, 1.0, 0.0)
        for side, factor in ((0, dpres[k]), (1, acts[k])):
            value = lax.dot_general(
                cols[:, side * block_rows : (side + 1) * block_rows],
                factor[...],
                dims,
                preferred_element_type=F32,
            )
            value += mine * both[side * block_rows : (side + 1) * block_rows]
            held[k, side] = value.astype(BF16)
        for copy in moves(k, ours[k], False):
            copy.start()

    @pl.when(elsewhere)
    def _():
        for copy in moves(group, hot, True):
            copy.wait()
        for side in range(2):
            value = held[group, side].astype(F32)
            value += both[side * block_rows : (side + 1) * block_rows]
            held[group, side] = value.astype(BF16)
        for copy in moves(group, hot, False):
            copy.start()
        for copy in moves(group, hot, False):
            copy.wait()

    for k in range(group):
        for copy in moves(k, ours[k], False):
            copy.wait()


def last_stage(ids, at, hot_index, cols, table, rows, chunks, totals):
    group = len(chunks)
    arrays = [block for chunk in chunks for block in chunk]
    hidden = rows.shape[1]
    block_rows = table.shape[1] // 2
    out_shape = jax.ShapeDtypeStruct(totals[0].shape, BF16)
    vmem = pl.BlockSpec(memory_space=pltpu.VMEM)
    hbm = pl.BlockSpec(memory_space=pltpu.HBM)
    return pl.pallas_call(
        functools.partial(last_body, group, at),
        in_specs=[pl.BlockSpec(memory_space=pltpu.SMEM)]
        + [vmem] * (3 + len(arrays))
        + [hbm, hbm],
        out_specs=[hbm, hbm],
        out_shape=[out_shape, out_shape],
        scratch_shapes=[
            pltpu.VMEM((group + 1, 2, block_rows, hidden), BF16),
            pltpu.VMEM((2 * block_rows, hidden), F32),
            pltpu.SemaphoreType.DMA((group + 1, 2)),
        ],
        input_output_aliases={4 + len(arrays): 0, 5 + len(arrays): 1},
        compiler_params=pltpu.CompilerParams(vmem_limit_bytes=16 * 2**20),
        cost_estimate=pl.CostEstimate(
            flops=8 * group * table.size * hidden,
            bytes_accessed=8 * group * block_rows * hidden,
            transcendentals=0,
        ),
        name="last_stage",
    )(
        jnp.concatenate([ids, hot_index[None]]),
        cols,
        table,
        rows,
        *[in_vmem(array) for array in arrays],
        *totals,
    )


def load_body(up_hbm, down_hbm, up_ref, down_ref, sems):
    copies = [
        pltpu.make_async_copy(up_hbm, up_ref, sems.at[0]),
        pltpu.make_async_copy(down_hbm, down_ref, sems.at[1]),
    ]
    for copy in copies:
        copy.start()
    for copy in copies:
        copy.wait()


def load(up_local, down_local):
    hbm, vmem = pl.BlockSpec(memory_space=pltpu.HBM), pl.BlockSpec(memory_space=pltpu.VMEM)
    return pl.pallas_call(
        load_body,
        in_specs=[hbm, hbm],
        out_specs=[vmem, vmem],
        out_shape=[
            jax.ShapeDtypeStruct(weights.shape, BF16) for weights in (up_local, down_local)
        ],
        scratch_shapes=[pltpu.SemaphoreType.DMA((2,))],
        compiler_params=pltpu.CompilerParams(vmem_limit_bytes=2**20),
        cost_estimate=pl.CostEstimate(
            flops=0, bytes_accessed=8 * up_local.size, transcendentals=0
        ),
        name="load",
    )(in_hbm(up_local), in_hbm(down_local))


def pick_rows(count, rows, want):
    have = lax.broadcasted_iota(jnp.int32, (count, rows), 1)
    return jnp.where(have == want, 1.0, 0.0).astype(BF16)


def ffn_body(planes, block, owner_ref, *refs):
    arrived = refs[:planes]
    up_ref, down_ref, chunk_ref, hot_ref, x_ref, g_ref = refs[planes:]
    rows = arrived[0].shape[0]
    mine = rows // (2 * HCAP) * CAP
    extra = rows // (2 * HCAP) * EXTRA
    normal, rest = planes * mine, planes * extra
    hidden = up_ref.shape[1]
    at = lax.broadcasted_iota(jnp.int32, (normal + rest, 1), 0)
    hot_at = at - normal
    is_hot = at >= normal
    plane = jnp.where(is_hot, hot_at // extra, at // mine)
    within = jnp.where(is_hot, hot_at % extra, at % mine)
    line = jnp.where(
        is_hot,
        within // EXTRA * (2 * HCAP) + CAP + within % EXTRA,
        within // CAP * (2 * HCAP) + within % CAP,
    )
    line = jnp.where(jnp.logical_and(is_hot, owner_ref[0] == 0), -2 * HCAP, line)
    for to_ref, shift in ((x_ref, 0), (g_ref, HCAP)):
        value = None
        for s in range(planes):
            pick = pick_rows(normal + rest, rows, jnp.where(plane == s, line + shift, -1))
            term = jnp.dot(pick, arrived[s][...], preferred_element_type=F32)
            value = term if value is None else value + term
        to_ref[...] = value.astype(BF16)
    for at in range(0, hidden, block):
        here = pl.ds(at, block)
        preact = jnp.dot(x_ref[...], up_ref[:, here], preferred_element_type=F32)
        value, slope = gelu_pair(preact)
        value = value.astype(BF16)
        chunk_ref[:normal, here] = value[:normal]
        hot_ref[:rest, here] = value[normal:]
        d_act = lax.dot_general(
            g_ref[...], down_ref[here, :], (((1,), (1,)), ((), ())), preferred_element_type=F32
        )
        d_pre = (d_act * slope).astype(BF16)
        chunk_ref[normal:, here] = d_pre[:normal]
        hot_ref[rest:, here] = d_pre[normal:]


def ffn(owner, arrived, up_held, down_held):
    planes = len(arrived)
    width, hidden = up_held.shape
    blocks = arrived[0].shape[0] // (2 * HCAP)
    normal, rest = planes * blocks * CAP, planes * blocks * EXTRA
    vmem = pl.BlockSpec(memory_space=pltpu.VMEM)
    return pl.pallas_call(
        functools.partial(ffn_body, planes, min(hidden, 256)),
        in_specs=[pl.BlockSpec(memory_space=pltpu.SMEM)] + [vmem] * (planes + 2),
        out_specs=[vmem, vmem],
        out_shape=[
            jax.ShapeDtypeStruct((2 * normal, hidden), BF16),
            jax.ShapeDtypeStruct((2 * rest, hidden), BF16),
        ],
        scratch_shapes=[pltpu.VMEM((normal + rest, width), BF16)] * 2,
        compiler_params=pltpu.CompilerParams(
            vmem_limit_bytes=12 * 2**20 + 16 * (normal + rest) * width
        ),
        cost_estimate=pl.CostEstimate(
            flops=4 * (normal + rest) * width * hidden,
            bytes_accessed=4 * width * hidden,
            transcendentals=2 * (normal + rest) * hidden,
        ),
        name="ffn",
    )(owner, *arrived, in_vmem(up_held), in_vmem(down_held))


def parts_body(block, chunk_ref, hot_ref, up_ref, down_ref, part_ref, act, dpre):
    normal, rest = chunk_ref.shape[0] // 2, hot_ref.shape[0] // 2
    planes = part_ref.shape[0]
    width = up_ref.shape[0]
    act[:normal], act[normal:] = chunk_ref[:normal], hot_ref[:rest]
    dpre[:normal], dpre[normal:] = chunk_ref[normal:], hot_ref[rest:]
    mine, extra = normal // planes, rest // planes

    def put(rows, here):
        for s in range(planes):
            part_ref[s, :mine, here] = rows[s * mine : (s + 1) * mine]
            part_ref[s, mine:, here] = rows[normal + s * extra : normal + (s + 1) * extra]

    for at in range(0, width, block):
        here = pl.ds(at, block)
        out = jnp.dot(act[...], down_ref[:, here], preferred_element_type=F32).astype(BF16)
        put(out, here)
        back = lax.dot_general(
            dpre[...], up_ref[here, :], (((1,), (1,)), ((), ())), preferred_element_type=F32
        ).astype(BF16)
        put(back, pl.ds(width + at, block))


def parts(planes, chunk, hot, up_local, down_local):
    width, hidden = up_local.shape
    rows = (chunk.shape[0] + hot.shape[0]) // 2
    vmem = pl.BlockSpec(memory_space=pltpu.VMEM)
    return pl.pallas_call(
        functools.partial(parts_body, 256),
        in_specs=[vmem] * 4,
        out_specs=vmem,
        out_shape=jax.ShapeDtypeStruct((planes, rows // planes, 2 * width), BF16),
        scratch_shapes=[pltpu.VMEM((rows, hidden), BF16)] * 2,
        compiler_params=pltpu.CompilerParams(vmem_limit_bytes=12 * 2**20),
        cost_estimate=pl.CostEstimate(
            flops=4 * rows * width * hidden,
            bytes_accessed=4 * width * hidden,
            transcendentals=0,
        ),
        name="parts",
    )(in_vmem(chunk), in_vmem(hot), in_vmem(up_local), in_vmem(down_local))


def back_body(count, piece_rows, piece_ref, *refs):
    parts_in, out_ref = refs[:-1], refs[-1]
    rows = parts_in[0].shape[0]
    width = out_ref.shape[1]
    slots = 2 * HCAP + piece_rows
    total = count * slots
    at = lax.broadcasted_iota(jnp.int32, (total, 1), 0)
    place, line = at // slots, at % slots
    within = line % HCAP
    row = jnp.where(
        within < CAP, place * CAP + within, count * CAP + place * EXTRA + within - CAP
    )
    outs = pick_rows(total, rows, jnp.where(line < HCAP, row, -1))
    backs = pick_rows(
        total, rows, jnp.where(jnp.logical_and(line >= HCAP, line < 2 * HCAP), row, -1)
    )
    pieces = pick_rows(total, piece_rows, line - 2 * HCAP)

    def summed(here):
        value = parts_in[0][:, here].astype(F32)
        for part in parts_in[1:]:
            value = value + part[:, here].astype(F32)
        return value.astype(BF16)

    block = 512
    for start in range(0, width, block):
        here, there = pl.ds(start, block), pl.ds(width + start, block)
        value = jnp.dot(outs, summed(here), preferred_element_type=F32)
        value += jnp.dot(backs, summed(there), preferred_element_type=F32)
        value += jnp.dot(pieces, piece_ref[:, here], preferred_element_type=F32)
        out_ref[:, here] = value.astype(BF16)


def back_rows(count, piece, parts_in):
    piece_rows, width = piece.shape
    slots = 2 * HCAP + piece_rows
    vmem = pl.BlockSpec(memory_space=pltpu.VMEM)
    return pl.pallas_call(
        functools.partial(back_body, count, piece_rows),
        in_specs=[vmem] * (1 + len(parts_in)),
        out_specs=vmem,
        out_shape=jax.ShapeDtypeStruct((count * slots, width), BF16),
        compiler_params=pltpu.CompilerParams(vmem_limit_bytes=24 * 2**20),
        cost_estimate=pl.CostEstimate(
            flops=8 * count * slots * parts_in[0].shape[0] * width,
            bytes_accessed=2 * count * slots * width,
            transcendentals=0,
        ),
        name="back_rows",
    )(piece, *parts_in).reshape(count, slots, width)


def combine_body(codes_ref, gates_ref, rows_ref, out_ref, back_ref):
    tokens, rows = out_ref.shape[0], rows_ref.shape[0]
    have = lax.broadcasted_iota(jnp.int32, (rows, tokens), 0)

    def pick(want):
        return jnp.where(have == want, 1.0, 0.0).astype(BF16)

    picks = [pick(codes_ref[c : c + 1, :]) for c in range(2)]
    back = pick(codes_ref[0:1, :] + HCAP) + pick(codes_ref[1:2, :] + HCAP)
    gates = jnp.transpose(gates_ref[...])
    take = (((0,), (0,)), ((), ()))
    width = out_ref.shape[1]
    block = 512
    for start in range(0, width, block):
        here = pl.ds(start, block)
        value = [
            lax.dot_general(pick, rows_ref[:, here], take, preferred_element_type=F32)
            for pick in picks
        ]
        out_ref[:, here] = (gates[:, 0:1] * value[0] + gates[:, 1:2] * value[1]).astype(BF16)
        back_ref[:, here] = lax.dot_general(
            back, rows_ref[:, here], take, preferred_element_type=F32
        ).astype(BF16)


def combine(codes, gates, rows):
    shape = jax.ShapeDtypeStruct((codes.shape[0], rows.shape[1]), BF16)
    vmem = pl.BlockSpec(memory_space=pltpu.VMEM)
    return pl.pallas_call(
        combine_body,
        in_specs=[vmem] * 3,
        out_specs=[vmem] * 2,
        out_shape=[shape, shape],
        compiler_params=pltpu.CompilerParams(vmem_limit_bytes=16 * 2**20),
        cost_estimate=pl.CostEstimate(
            flops=6 * rows.size * codes.shape[0], bytes_accessed=6 * rows.size, transcendentals=0
        ),
        name="combine",
    )(jnp.pad(codes.T, ((0, 6), (0, 0))), jnp.pad(gates.T, ((0, 6), (0, 0))), rows)


def pack_body(mask_ref, *refs):
    from_refs, (out_ref, normal_ref), (*to_refs, sems) = refs[:5], refs[5:7], refs[7:]
    copies = [
        pltpu.make_async_copy(a, b, sems.at[k]) for k, (a, b) in enumerate(zip(from_refs, to_refs))
    ]
    for copy in copies:
        copy.start()
    for copy in copies:
        copy.wait()
    ids_ref, slots_ref, gates_ref, tokens_ref, grad_ref = to_refs
    hot_index = 0
    for e in range(mask_ref.shape[0]):
        hot_index = jnp.where(mask_ref[e] > 0, e, hot_index)
    ids, route_slots = ids_ref[...], slots_ref[...]
    kept = route_slots < CAP
    normal_codes = jnp.where(kept, ids * CAP + route_slots, -2)
    extra = jnp.logical_and(ids == hot_index, jnp.logical_not(kept))
    hot_codes = jnp.where(extra, route_slots, -2)
    rows, tokens = out_ref.shape[0], tokens_ref.shape[0]
    at = lax.broadcasted_iota(jnp.int32, (rows, 1), 0)
    slots = 2 * HCAP
    line = at % slots
    within = line % HCAP
    normal = jnp.where(within < CAP, at // slots * CAP + within, -1)
    hot = jnp.where(within < CAP, -1, within)
    picks = jnp.zeros((rows, tokens), F32)
    gates = jnp.zeros((rows, 1), F32)
    count = normal_ref.shape[1]
    normal_at = lax.broadcasted_iota(jnp.int32, (count, 1), 0)
    normal_picks = jnp.zeros((count, tokens), F32)
    normal_gates = jnp.zeros((count, 1), F32)
    for c in range(2):
        gate = gates_ref[c : c + 1, :]
        to_normal, to_hot = normal_codes[c : c + 1, :], hot_codes[c : c + 1, :]
        pick = jnp.logical_or(to_normal == normal, to_hot == hot)
        picks += jnp.where(pick, 1.0, 0.0)
        gates += jnp.sum(jnp.where(pick, gate, 0.0), axis=1, keepdims=True)
        pick = to_normal == normal_at
        normal_picks += jnp.where(pick, 1.0, 0.0)
        normal_gates += jnp.sum(jnp.where(pick, gate, 0.0), axis=1, keepdims=True)
    picks_x = jnp.where(line < HCAP, picks, 0.0).astype(BF16)
    picks_g = jnp.where(line < HCAP, 0.0, picks).astype(BF16)
    normal_picks = normal_picks.astype(BF16)
    width = out_ref.shape[1]
    block = 512
    for start in range(0, width, block):
        here = pl.ds(start, block)
        x, g = tokens_ref[:, here], grad_ref[:, here]
        value = jnp.dot(picks_x, x, preferred_element_type=F32)
        value += gates * jnp.dot(picks_g, g, preferred_element_type=F32)
        out_ref[:, here] = value.astype(BF16)
        normal_ref[0, :, here] = jnp.dot(normal_picks, x, preferred_element_type=F32).astype(BF16)
        normal_ref[1, :, here] = (
            normal_gates * jnp.dot(normal_picks, g, preferred_element_type=F32)
        ).astype(BF16)


def pack(count, mask, ids, route_slots, gates, tokens, cotangent):
    width = tokens.shape[1]
    vmem = pl.BlockSpec(memory_space=pltpu.VMEM)
    slots = 2 * HCAP
    rows = count * (slots + 2 * CAP)
    arrays = (ids, route_slots, gates, tokens, cotangent)
    return pl.pallas_call(
        pack_body,
        in_specs=[pl.BlockSpec(memory_space=pltpu.SMEM)]
        + [pl.BlockSpec(memory_space=pltpu.HBM)] * 5,
        out_specs=[vmem] * 2,
        out_shape=[
            jax.ShapeDtypeStruct((count * slots, width), BF16),
            jax.ShapeDtypeStruct((2, count * CAP, width), BF16),
        ],
        scratch_shapes=[pltpu.VMEM(array.shape, array.dtype) for array in arrays]
        + [pltpu.SemaphoreType.DMA((len(arrays),))],
        compiler_params=pltpu.CompilerParams(vmem_limit_bytes=16 * 2**20),
        cost_estimate=pl.CostEstimate(
            flops=4 * rows * tokens.size, bytes_accessed=2 * rows * width, transcendentals=0
        ),
        name="pack",
    )(mask, *[in_hbm(array) for array in arrays])


def on_device(tokens, cotangent, gate_probs, expert_ids, route_slots, hot_mask, w_up, w_down):
    count = lax.axis_size("expert")
    planes = lax.axis_size("dp")
    index = lax.axis_index("expert")
    model_width = tokens.shape[1]
    up_local = w_up[0]
    down_local = w_down[0]
    hidden = up_local.shape[1]
    block_rows = model_width // count
    buffers = count * CAP
    swap = flip_bit(count, 1)
    codes = jnp.arange(count, dtype=jnp.int32)
    hot_index = jnp.sum(hot_mask * codes).astype(jnp.int32)
    owner = (hot_index == index).astype(jnp.int32)[None]
    sources = ring_sources(count)

    hot_extra = jnp.logical_and(
        expert_ids == hot_index, jnp.logical_and(route_slots >= CAP, route_slots < HCAP)
    )
    kept_normal = route_slots < CAP
    rows, normal_rows = pack(
        count, hot_mask, expert_ids.T, route_slots.T, gate_probs.T, tokens, cotangent
    )

    def exchange(value):
        return lax.all_to_all(value, "expert", split_axis=0, concat_axis=0, tiled=True)

    slots = 2 * HCAP
    arrived = exchange(rows.reshape(count, slots, model_width))
    arrived = gather_planes(arrived.reshape(count * slots, model_width))
    up_held, down_held = load(up_local, down_local)
    chunk, hot_factors = ffn(
        owner, arrived, up_held, down_held
    )
    hot_rows_count = hot_factors.shape[0] // 2

    chunks = ring_gather(chunk)

    part = parts(planes, chunk, hot_factors, up_held, down_held)
    part, *arrived = lax.optimization_barrier((part, *arrived))

    both = normal_rows.reshape(2, buffers, count, block_rows)
    both = jnp.transpose(jnp.concatenate([both[0], both[1]], axis=2), (1, 0, 2))
    columns = exchange(both)
    part, columns = lax.optimization_barrier((part, columns))
    columns = gather_planes(columns)
    place = jnp.arange(count * buffers, dtype=jnp.int32)
    turned = (place // CAP % count * count + place // buffers) * CAP + place % CAP
    turn = (turned[:, None] == place[None, :]).astype(BF16)
    cols = jnp.concatenate(
        [
            matmul(turn, block.reshape(count * buffers, 2 * block_rows))
            .astype(BF16)
            .reshape(count, buffers, 2 * block_rows)
            for block in columns
        ],
        axis=1,
    )

    received = [part[0]] + [dp_shift(part[s], s) for s in range(1, planes)]
    pieces = exchange(hot_factors.reshape(count, -1, model_width))
    piece = lax.dynamic_index_in_dim(pieces, hot_index, 0, keepdims=False)
    returned = back_rows(count, piece, received)
    returned = exchange(returned)
    back_slots = returned.shape[1]
    came = jnp.where(
        jnp.logical_or(kept_normal, hot_extra), expert_ids * back_slots + route_slots, -HCAP - 1
    )
    layer_out, grad_tokens = combine(
        came, gate_probs, returned.reshape(count * back_slots, model_width)
    )

    out_shape = jax.ShapeDtypeStruct((count, block_rows, hidden), BF16)
    totals = None
    at = 0
    groups = ring_groups(count)
    for k, group in enumerate(groups):
        mine = [chunks[d] for d in group]
        others = [[send(block, swap) for block in chunk] for chunk in mine]
        if k + 1 == len(groups):
            break
        totals = grad_stage(sources, at, cols, mine + others, totals, out_shape)
        at += 2 * len(group)

    hot_rows = returned[:, 2 * HCAP :].reshape(-1, hidden)
    held = jnp.concatenate(
        [
            lax.dynamic_slice_in_dim(block, index * block_rows, block_rows, 1)
            for block in arrived
        ]
    )
    hot_at = jnp.arange(hot_rows_count, dtype=jnp.int32)
    line = hot_at // EXTRA * slots + CAP + hot_at % EXTRA
    line_codes = jnp.arange(planes * count * slots, dtype=jnp.int32)
    none = jnp.full((hot_rows_count,), -1, jnp.int32)

    def pick_columns(want):
        return matmul((want[:, None] == line_codes[None, :]).astype(BF16), held).astype(BF16)

    table = jnp.concatenate(
        [
            pick_columns(jnp.concatenate([none, line])),
            pick_columns(jnp.concatenate([line + HCAP, none])),
        ],
        axis=1,
    )
    grad_up, grad_down = last_stage(
        sources, at, hot_index, cols, table, hot_rows, mine + others, totals
    )
    return (layer_out, grad_tokens, grad_up, grad_down)


def solution(mesh):
    placed = (
        P(("dp", "expert"), None),
        P(("dp", "expert"), None),
        P(("dp", "expert"), None),
        P(("dp", "expert"), None),
        P(("dp", "expert"), None),
        P(),
        P("expert", None, "dp"),
        P("expert", "dp", None),
    )

    return jax.shard_map(
        on_device,
        mesh=mesh,
        in_specs=placed,
        out_specs=(
            P(("dp", "expert"), None),
            P(("dp", "expert"), None),
            P(None, "expert", "dp"),
            P(None, "expert", "dp"),
        ),
        check_vma=False,
    )
```

time: 193 us -> 155 us (0.80)
  local copies, waits for them, and re-layouts: 18.5 us -> 3.66 us
  other arithmetic: 12.5 us -> 2.82 us
  waiting for transfers between devices: 56 us -> 49 us
  starting transfers between devices: 38.3 us -> 31.6 us
  Pallas kernels: 37.7 us -> 41.8 us
  matrix products: 4.08 us -> 1.13 us
    ppermute x3, waiting for transfers between devices: 16.9 us -> 0.01 us  [dp_shift(): lax.ppermute(value, 'dp', [(p, (p + shift) % count) for p in range(count)])]
    ppermute x17, waiting for transfers between devices: 28.2 us -> 39 us  [send(): return lax.ppermute(value, 'expert', pairs)]
    pallas_call x2 -> x6, Pallas kernels: 11.1 us -> 20.2 us  [the longest x1 5.79 us: load(): pl.pallas_call(load_body, in_specs=[hbm, hbm], out_specs=[vmem, vmem], ou...]
    pallas_call x5 -> x4, Pallas kernels: 22.6 us -> 16.6 us  [grad_stage(): pl.pallas_call(functools.partial(grad_body, layout, first), grid_spec=plt...]
    ppermute x17, starting transfers between devices: 17.7 us -> 13 us  [send(): return lax.ppermute(value, 'expert', pairs)]
    slice x7 -> x0, local copies, waits for them, and re-layouts: 3.86 us -> none  [the longest x1 1.47 us: on_device(): returned[:, CAP:]]
    squeeze x4, local copies, waits for them, and re-layouts: 4.98 us -> 1.71 us  [the longest x1 0.88 us: on_device(): received = [part[0]] + [dp_shift(part[s], s) for s in range(1, planes)]]
    reshape x8 -> x1, local copies, waits for them, and re-layouts: 3.29 us -> 0.03 us  [on_device(): hot_rows = returned[:, 2 * HCAP:].reshape(-1, hidden)]
  transfers between devices with their start and end apart: 23 -> 23, of which waited for: 5 -> 4; matrix products, arithmetic and copies ran while one was open for 12% -> 4% of each run, Pallas kernels for 14% -> 24%
where the time goes in v1:
time: 155 us; the launch traced here: 154 us
  waiting for transfers between devices  49 us (32%)
  Pallas kernels  41.8 us (27%)
  starting transfers between devices  31.6 us (20%)
  blocking collectives  19.9 us (13%)
  between operations  3.69 us (2%)
  local copies, waits for them, and re-layouts  3.66 us (2%)
  other arithmetic  2.82 us (2%)
    ppermute x17, waiting for transfers between devices, send(): return lax.ppermute(value, 'expert', pairs)  39 us
    all_to_all x1, blocking collectives, exchange(): lax.all_to_all(value, 'expert', split_axis=0, concat_axis=0, tiled=True)  19.9 us
    all_to_all x3, starting transfers between devices, exchange(): lax.all_to_all(value, 'expert', split_axis=0, concat_axis=0, tiled=True)  16.9 us
    pallas_call x4, Pallas kernels, grad_stage(): pl.pallas_call(functools.partial(grad_body, layout, first), grid_spec=plt...  16.6 us
    ppermute x17, starting transfers between devices, send(): return lax.ppermute(value, 'expert', pairs)  13 us
    all_to_all x3, waiting for transfers between devices, exchange(): lax.all_to_all(value, 'expert', split_axis=0, concat_axis=0, tiled=True)  9.94 us
    pallas_call x1, Pallas kernels, load(): pl.pallas_call(load_body, in_specs=[hbm, hbm], out_specs=[vmem, vmem], ou...  5.79 us
    pallas_call x1, Pallas kernels, ffn(): pl.pallas_call(functools.partial(ffn_body, planes, min(hidden, 256)), in_...  5.34 us
  transfers between devices with their start and end apart: 23, of which 4 were waited for; matrix products, arithmetic and copies ran while one was open for 4% of the time, Pallas kernels for 24%

profile of v1, /device:TPU:11, one launch (start us, length us, event | category | flops | bytes accessed | tf_op | source)
XLA Modules:
  0.0 153.6 jit_solution(1355625676946394785)
XLA Ops:
  1.3 2.5 %pack.1 = (bf16[128,2048]{1,0:T(8,128)(2,1)S(1)}, bf16[2,32,2048]{2,1,0:T(8,128)(2,1)S(1)}) custom-call(s32[16]{0:T(128)S(1)} %copy-done.2, s32[2,128]{1,0:T(2,128)} %bitcast.51, s32[2,128]{1,0:T(2,128)} %bitcast.50, f32[2,128]{1,0:T(2,128)} %bitcast.52, bf16[128,2048]{1,0:T(8,128)(2,1)} %refs_3_.1, bf16[128,2048]{1,0:T(8,128)(2,1)} %refs_4_.1), custom_call_target="tpu_custom_call" | custom-call | flops 201326592 | bytes 786432 | tf_op jit(solution)/shard_map/pack/pallas_call | solution.py:573
  3.8 19.9 %all_to_all.20 = bf16[16,8,2048]{2,1,0:T(8,128)(2,1)S(1)} all-to-all(bf16[16,8,2048]{2,1,0:T(8,128)(2,1)S(1)} %bitcast.42), channel_id=1, replica_groups=mesh['dp'=2,'expert'=16] {'expert'}, dimensions={0} | all-to-all | bytes 1048576 | tf_op jit(solution)/shard_map/all_to_all | solution.py:617
  25.8 5.1 %all-to-all-start.2 = ((bf16[16,32,256]{2,1,0:T(8,128)(2,1)}), bf16[16,32,256]{2,1,0:T(8,128)(2,1)S(1)}, u32[]{:S(2)}, u32[]{:S(2)}) async-start(bf16[16,32,256]{2,1,0:T(8,128)(2,1)} %maximum_bitcast_fusion), calls=%async_computation.2 | async-start | bytes 524288 | tf_op jit(solution)/shard_map/all_to_all | solution.py:617
  32.2 5.8 %load.1 = (bf16[2048,2048]{1,0:T(8,128)(2,1)S(1)}, bf16[2048,2048]{1,0:T(8,128)(2,1)S(1)}) custom-call(bf16[2048,2048]{1,0:T(8,128)(2,1)} %bitcast.43, bf16[2048,2048]{1,0:T(8,128)(2,1)} %bitcast.44), custom_call_target="tpu_custom_call" | custom-call | bytes 33554432 | tf_op jit(solution)/shard_map/load/pallas_call | solution.py:285
  38.0 5.3 %ffn.1 = (bf16[128,2048]{1,0:T(8,128)(2,1)S(1)}, bf16[128,2048]{1,0:T(8,128)(2,1)}) custom-call(s32[1]{0:T(128)} %bitcast.2.owner_ref, bf16[128,2048]{1,0:T(8,128)(2,1)S(1)} %bitcast.40, bf16[128,2048]{1,0:T(8,128)(2,1)S(1)} %collective-permute-done.refs_1_, bf16[2048,2048]{1,0:T(8,128)(2,1)S(1)} %get-tuple-element.28.refs_2_.up_ref, ...), custom_call_target="tpu_custom_call" | custom-call | flops 2147483648 | bytes 16777216 | tf_op jit(solution)/shard_map/ffn/pallas_call | solution.py:353
  43.4 5.0 %parts.1 = bf16[2,64,4096]{2,1,0:T(8,128)(2,1)S(1)} custom-call(bf16[128,2048]{1,0:T(8,128)(2,1)S(1)} %get-tuple-element.31.chunk_ref.refs_0_, bf16[128,2048]{1,0:T(8,128)(2,1)} %get-tuple-element.30.hot_ref, bf16[2048,2048]{1,0:T(8,128)(2,1)S(1)} %get-tuple-element.28.refs_2_.up_ref, bf16[2048,2048]{1,0:T(8,128)(2,1)S(1)} %get-tuple-element.29.refs_3_.down_ref), custom_call_target="tpu_custom_call" | custom-call | flops 2147483648 | bytes 16777216 | tf_op jit(solution)/shard_map/parts/pallas_call | solution.py:401
  48.5 6.0 %all-to-all-start.1 = ((bf16[16,8,2048]{2,1,0:T(8,128)(2,1)}), bf16[16,8,2048]{2,1,0:T(8,128)(2,1)}, u32[]{:S(2)}, u32[]{:S(2)}) async-start(bf16[16,8,2048]{2,1,0:T(8,128)(2,1)} %bitcast.9), calls=%async_computation.1 | async-start | bytes 1048576 | tf_op jit(solution)/shard_map/all_to_all | solution.py:617
  59.1 9.9 %all-to-all-done.1 = bf16[16,8,2048]{2,1,0:T(8,128)(2,1)} async-done(((bf16[16,8,2048]{2,1,0:T(8,128)(2,1)}), bf16[16,8,2048]{2,1,0:T(8,128)(2,1)}, u32[]{:S(2)}, u32[]{:S(2)}) %all-to-all-start.1) | async-done | bytes 524320 | tf_op jit(solution)/shard_map/all_to_all | solution.py:617
  69.8 2.0 %back_rows.1 = bf16[256,2048]{1,0:T(8,128)(2,1)} custom-call(bf16[8,2048]{1,0:T(8,128)(2,1)S(1)} %dynamic-slice_bitcast_fusion.piece_ref, bf16[64,4096]{1,0:T(8,128)(2,1)S(1)} %get-tuple-element.51.refs_0_, bf16[64,4096]{1,0:T(8,128)(2,1)S(1)} %collective-permute-done.1.refs_1_), custom_call_target="tpu_custom_call" | custom-call | flops 268435456 | bytes 1048576 | tf_op jit(solution)/shard_map/back_rows/pallas_call | solution.py:454
  71.7 5.7 %all-to-all-start.3 = ((bf16[16,16,2048]{2,1,0:T(8,128)(2,1)}), bf16[16,16,2048]{2,1,0:T(8,128)(2,1)S(1)}, u32[]{:S(2)}, u32[]{:S(2)}) async-start(bf16[16,16,2048]{2,1,0:T(8,128)(2,1)} %bitcast.14), calls=%async_computation.3 | async-start | bytes 2097152 | tf_op jit(solution)/shard_map/all_to_all | solution.py:617
  79.0 1.5 collective-permute-start.8
  80.6 1.6 %collective-permute-start.19 = (bf16[128,2048]{1,0:T(8,128)(2,1)S(1)}, bf16[128,2048]{1,0:T(8,128)(2,1)S(1)}, u32[]{:S(2)}, u32[]{:S(2)}) collective-permute-start(bf16[128,2048]{1,0:T(8,128)(2,1)S(1)} %get-tuple-element.31.chunk_ref.refs_0_), channel_id=1, source_target_pairs={{0,1},{1,0},{2,3},{3,2},{4,5},{5,4},{6,7},{7,6},{8,9},{9,8},{10,11... | collective-permute-start | bytes 1572872 | tf_op jit(solution)/shard_map/ppermute | solution.py:53
  83.8 29.6 %collective-permute-done.4.refs_0_ = bf16[128,2048]{1,0:T(8,128)(2,1)} collective-permute-done((bf16[128,2048]{1,0:T(8,128)(2,1)S(1)}, bf16[128,2048]{1,0:T(8,128)(2,1)}, u32[]{:S(2)}, u32[]{:S(2)}) %collective-permute-start.4) | collective-permute-done | bytes 524320 | tf_op jit(solution)/shard_map/ppermute | solution.py:53
  113.4 1.5 collective-permute-start.9
  114.9 1.6 %collective-permute-start.18 = (bf16[128,2048]{1,0:T(8,128)(2,1)}, bf16[128,2048]{1,0:T(8,128)(2,1)S(1)}, u32[]{:S(2)}, u32[]{:S(2)}) collective-permute-start(bf16[128,2048]{1,0:T(8,128)(2,1)} %collective-permute-done.7.refs_1_), channel_id=1, source_target_pairs={{0,1},{1,0},{2,3},{3,2},{4,5},{5,4},{6,7},{7,6},{8,9},{9,8},{10,11... | collective-permute-start | bytes 1572872 | tf_op jit(solution)/shard_map/ppermute | solution.py:53
  117.5 8.6 %collective-permute-done.5.refs_0_ = bf16[128,2048]{1,0:T(8,128)(2,1)S(1)} collective-permute-done((bf16[128,2048]{1,0:T(8,128)(2,1)}, bf16[128,2048]{1,0:T(8,128)(2,1)S(1)}, u32[]{:S(2)}, u32[]{:S(2)}) %collective-permute-start.5) | collective-permute-done | bytes 524320 | tf_op jit(solution)/shard_map/ppermute | solution.py:53
  126.1 1.8 %collective-permute-start.13 = (bf16[128,2048]{1,0:T(8,128)(2,1)S(1)}, bf16[128,2048]{1,0:T(8,128)(2,1)S(1)}, u32[]{:S(2)}, u32[]{:S(2)}) collective-permute-start(bf16[128,2048]{1,0:T(8,128)(2,1)S(1)} %collective-permute-done.5.refs_0_), channel_id=1, source_target_pairs={{0,1},{1,0},{2,3},{3,2},{4,5},{5,4},{6,7},{7,6},{8,9},{9,8},{10,11... | collective-permute-start | bytes 1572872 | tf_op jit(solution)/shard_map/ppermute | solution.py:53
  128.1 1.7 %collective-permute-start.10 = (bf16[64,2048]{1,0:T(8,128)(2,1)S(1)}, bf16[64,2048]{1,0:T(8,128)(2,1)S(1)}, u32[]{:S(2)}, u32[]{:S(2)}) collective-permute-start(bf16[64,2048]{1,0:T(8,128)(2,1)S(1)} %slice.32), channel_id=1, source_target_pairs={{0,2},{1,3},{4,0},{5,1},{8,4},{9,5},{12,8},{13,9},{14,12},{15,13},... | collective-permute-start | bytes 786440 | tf_op jit(solution)/shard_map/ppermute | solution.py:53
  130.2 2.5 %grad_stage.4 = (bf16[16,128,2048]{2,1,0:T(8,128)(2,1)}, bf16[16,128,2048]{2,1,0:T(8,128)(2,1)}) custom-call(s32[16]{0:T(128)S(1)} %fusion.22.ids_ref, bf16[16,64,256]{2,1,0:T(8,128)(2,1)S(1)} %pad_maximum_fusion.cols_ref, bf16[128,2048]{1,0:T(8,128)(2,1)S(1)} %get-tuple-element.31.chunk_ref.refs_0_, bf16[128,2048]{1,0:T(8,128)(2,1)S(1)} %collective-permute-done.19.refs_1_), custom_call_target="tpu_custom_call" | custom-call | flops 134217728 | bytes 3145728 | tf_op jit(solution)/shard_map/grad_stage/pallas_call | solution.py:150
  133.8 5.0 %grad_stage.5 = (bf16[16,128,2048]{2,1,0:T(8,128)(2,1)}, bf16[16,128,2048]{2,1,0:T(8,128)(2,1)}) custom-call(s32[16]{0:T(128)S(1)} %fusion.22.ids_ref, bf16[16,64,256]{2,1,0:T(8,128)(2,1)S(1)} %pad_maximum_fusion.cols_ref, bf16[128,2048]{1,0:T(8,128)(2,1)S(1)} %copy-done.1, ...), custom_call_target="tpu_custom_call", output_to_operand_aliasing={{0}: (6, {}), {1}: (7, {})} | custom-call | flops 268435456 | bytes 6291456 | tf_op jit(solution)/shard_map/grad_stage/pallas_call | solution.py:150
  138.7 5.2 %grad_stage.6 = (bf16[16,128,2048]{2,1,0:T(8,128)(2,1)}, bf16[16,128,2048]{2,1,0:T(8,128)(2,1)}) custom-call(s32[16]{0:T(128)S(1)} %fusion.22.ids_ref, bf16[16,64,256]{2,1,0:T(8,128)(2,1)S(1)} %pad_maximum_fusion.cols_ref, bf16[128,2048]{1,0:T(8,128)(2,1)} %collective-permute-done.4.refs_0_, ...), custom_call_target="tpu_custom_call", output_to_operand_aliasing={{0}: (6, {}), {1}: (7, {})} | custom-call | flops 268435456 | bytes 6291456 | tf_op jit(solution)/shard_map/grad_stage/pallas_call | solution.py:150
  144.8 4.0 %grad_stage.7 = (bf16[16,128,2048]{2,1,0:T(8,128)(2,1)}, bf16[16,128,2048]{2,1,0:T(8,128)(2,1)}) custom-call(s32[16]{0:T(128)S(1)} %fusion.22.ids_ref, bf16[16,64,256]{2,1,0:T(8,128)(2,1)S(1)} %pad_maximum_fusion.cols_ref, bf16[128,2048]{1,0:T(8,128)(2,1)S(1)} %collective-permute-done.5.refs_0_, ...), custom_call_target="tpu_custom_call", output_to_operand_aliasing={{0}: (6, {}), {1}: (7, {})} | custom-call | flops 268435456 | bytes 6291456 | tf_op jit(solution)/shard_map/grad_stage/pallas_call | solution.py:150
  148.8 1.6 %combine.1 = (bf16[128,2048]{1,0:T(8,128)(2,1)}, bf16[128,2048]{1,0:T(8,128)(2,1)}) custom-call(s32[8,128]{1,0:T(8,128)S(1)} %pad.10.codes_ref, f32[8,128]{1,0:T(8,128)S(1)} %pad.11.gates_ref, bf16[256,2048]{1,0:T(8,128)(2,1)S(1)} %bitcast.38), custom_call_target="tpu_custom_call" | custom-call | flops 402653184 | bytes 3145728 | tf_op jit(solution)/shard_map/combine/pallas_call | solution.py:497
  150.5 3.0 %last_stage.1 = (bf16[16,128,2048]{2,1,0:T(8,128)(2,1)}, bf16[16,128,2048]{2,1,0:T(8,128)(2,1)}) custom-call(s32[17]{0:T(128)S(1)} %pad_add_fusion.ids_ref, bf16[16,64,256]{2,1,0:T(8,128)(2,1)S(1)} %pad_maximum_fusion.cols_ref, bf16[128,256]{1,0:T(8,128)(2,1)S(1)} %pad_maximum_fusion.2.table_ref, ...), custom_call_target="tpu_custom_call", output_to_operand_aliasing={{0}: (8, {}), {1}: (9, {})} | custom-call | flops 1073741824 | bytes 4194304 | tf_op jit(solution)/shard_map/last_stage/pallas_call | solution.py:242
  (78 shorter events, 13.5 us)
Async XLA Ops:
  23.7 14.4 %collective-permute-start = (bf16[128,2048]{1,0:T(8,128)(2,1)S(1)}, bf16[128,2048]{1,0:T(8,128)(2,1)S(1)}, u32[]{:S(2)}, u32[]{:S(2)}) collective-permute-start(bf16[128,2048]{1,0:T(8,128)(2,1)S(1)} %bitcast.39), channel_id=1, source_target_pairs={{0,16},{16,0},{1,17},{17,1},{2,18},{18,2},{3,19},{19,3},{4,20},{20... | collective-permute-start | bytes 1572872 | tf_op jit(solution)/shard_map/ppermute | solution.py:58
  25.8 22.7 %all-to-all-start.2 = ((bf16[16,32,256]{2,1,0:T(8,128)(2,1)}), bf16[16,32,256]{2,1,0:T(8,128)(2,1)S(1)}, u32[]{:S(2)}, u32[]{:S(2)}) async-start(bf16[16,32,256]{2,1,0:T(8,128)(2,1)} %maximum_bitcast_fusion), calls=%async_computation.2 | async-start | bytes 524288 | tf_op jit(solution)/shard_map/all_to_all | solution.py:617
  48.5 20.5 %all-to-all-start.1 = ((bf16[16,8,2048]{2,1,0:T(8,128)(2,1)}), bf16[16,8,2048]{2,1,0:T(8,128)(2,1)}, u32[]{:S(2)}, u32[]{:S(2)}) async-start(bf16[16,8,2048]{2,1,0:T(8,128)(2,1)} %bitcast.9), calls=%async_computation.1 | async-start | bytes 1048576 | tf_op jit(solution)/shard_map/all_to_all | solution.py:617
  55.3 14.4 %collective-permute-start.1 = (bf16[64,4096]{1,0:T(8,128)(2,1)}, bf16[64,4096]{1,0:T(8,128)(2,1)S(1)}, u32[]{:S(2)}, u32[]{:S(2)}) collective-permute-start(bf16[64,4096]{1,0:T(8,128)(2,1)} %get-tuple-element.50), channel_id=1, source_target_pairs={{0,16},{16,0},{1,17},{17,1},{2,18},{18,2},{3,19},{19,3},{4,20},{20... | collective-permute-start | bytes 1572872 | tf_op jit(solution)/shard_map/ppermute | solution.py:58
  57.5 21.4 %collective-permute-start.3 = (bf16[128,2048]{1,0:T(8,128)(2,1)S(1)}, bf16[128,2048]{1,0:T(8,128)(2,1)S(1)}, u32[]{:S(2)}, u32[]{:S(2)}) collective-permute-start(bf16[128,2048]{1,0:T(8,128)(2,1)S(1)} %get-tuple-element.31.chunk_ref.refs_0_), channel_id=1, source_target_pairs={{0,4},{1,5},{4,8},{5,9},{8,12},{9,13},{12,14},{13,15},{14,10},{15,... | collective-permute-start | bytes 1572872 | tf_op jit(solution)/shard_map/ppermute | solution.py:53
  57.9 21.1 %collective-permute-start.7 = (bf16[128,2048]{1,0:T(8,128)(2,1)S(1)}, bf16[128,2048]{1,0:T(8,128)(2,1)}, u32[]{:S(2)}, u32[]{:S(2)}) collective-permute-start(bf16[128,2048]{1,0:T(8,128)(2,1)S(1)} %get-tuple-element.31.chunk_ref.refs_0_), channel_id=1, source_target_pairs={{0,2},{1,3},{4,0},{5,1},{8,4},{9,5},{12,8},{13,9},{14,12},{15,13},... | collective-permute-start | bytes 1572872 | tf_op jit(solution)/shard_map/ppermute | solution.py:53
  71.7 77.0 %all-to-all-start.3 = ((bf16[16,16,2048]{2,1,0:T(8,128)(2,1)}), bf16[16,16,2048]{2,1,0:T(8,128)(2,1)S(1)}, u32[]{:S(2)}, u32[]{:S(2)}) async-start(bf16[16,16,2048]{2,1,0:T(8,128)(2,1)} %bitcast.14), calls=%async_computation.3 | async-start | bytes 2097152 | tf_op jit(solution)/shard_map/all_to_all | solution.py:617
  79.0 51.2 %copy-start = (bf16[128,2048]{1,0:T(8,128)(2,1)}, bf16[128,2048]{1,0:T(8,128)(2,1)S(1)}, u32[]{:S(2)}) copy-start(bf16[128,2048]{1,0:T(8,128)(2,1)S(1)} %collective-permute-done.3.refs_0_) | copy-start | bytes 1572868
  79.0 34.4 %collective-permute-start.4 = (bf16[128,2048]{1,0:T(8,128)(2,1)S(1)}, bf16[128,2048]{1,0:T(8,128)(2,1)}, u32[]{:S(2)}, u32[]{:S(2)}) collective-permute-start(bf16[128,2048]{1,0:T(8,128)(2,1)S(1)} %collective-permute-done.3.refs_0_), channel_id=1, source_target_pairs={{0,4},{1,5},{4,8},{5,9},{8,12},{9,13},{12,14},{13,15},{14,10},{15,... | collective-permute-start | bytes 1572872 | tf_op jit(solution)/shard_map/ppermute | solution.py:53
  79.0 34.4 %collective-permute-start.8 = (bf16[128,2048]{1,0:T(8,128)(2,1)}, bf16[128,2048]{1,0:T(8,128)(2,1)}, u32[]{:S(2)}, u32[]{:S(2)}) collective-permute-start(bf16[128,2048]{1,0:T(8,128)(2,1)} %collective-permute-done.7.refs_1_), channel_id=1, source_target_pairs={{0,2},{1,3},{4,0},{5,1},{8,4},{9,5},{12,8},{13,9},{14,12},{15,13},... | collective-permute-start | bytes 1572872 | tf_op jit(solution)/shard_map/ppermute | solution.py:53
  80.6 35.9 %collective-permute-start.19 = (bf16[128,2048]{1,0:T(8,128)(2,1)S(1)}, bf16[128,2048]{1,0:T(8,128)(2,1)S(1)}, u32[]{:S(2)}, u32[]{:S(2)}) collective-permute-start(bf16[128,2048]{1,0:T(8,128)(2,1)S(1)} %get-tuple-element.31.chunk_ref.refs_0_), channel_id=1, source_target_pairs={{0,1},{1,0},{2,3},{3,2},{4,5},{5,4},{6,7},{7,6},{8,9},{9,8},{10,11... | collective-permute-start | bytes 1572872 | tf_op jit(solution)/shard_map/ppermute | solution.py:53
  82.9 32.0 %collective-permute-start.2 = (bf16[16,32,256]{2,1,0:T(8,128)(2,1)S(1)}, bf16[16,32,256]{2,1,0:T(8,128)(2,1)S(1)}, u32[]{:S(2)}, u32[]{:S(2)}) collective-permute-start(bf16[16,32,256]{2,1,0:T(8,128)(2,1)S(1)} %all-to-all-done.2), channel_id=1, source_target_pairs={{0,16},{16,0},{1,17},{17,1},{2,18},{18,2},{3,19},{19,3},{4,20},{20... | collective-permute-start | bytes 786440 | tf_op jit(solution)/shard_map/ppermute | solution.py:58
  83.1 33.6 %collective-permute-start.17 = (bf16[128,2048]{1,0:T(8,128)(2,1)S(1)}, bf16[128,2048]{1,0:T(8,128)(2,1)S(1)}, u32[]{:S(2)}, u32[]{:S(2)}) collective-permute-start(bf16[128,2048]{1,0:T(8,128)(2,1)S(1)} %collective-permute-done.3.refs_0_), channel_id=1, source_target_pairs={{0,1},{1,0},{2,3},{3,2},{4,5},{5,4},{6,7},{7,6},{8,9},{9,8},{10,11... | collective-permute-start | bytes 1572872 | tf_op jit(solution)/shard_map/ppermute | solution.py:53
  113.4 12.7 %collective-permute-start.5 = (bf16[128,2048]{1,0:T(8,128)(2,1)}, bf16[128,2048]{1,0:T(8,128)(2,1)S(1)}, u32[]{:S(2)}, u32[]{:S(2)}) collective-permute-start(bf16[128,2048]{1,0:T(8,128)(2,1)} %collective-permute-done.4.refs_0_), channel_id=1, source_target_pairs={{0,4},{1,5},{4,8},{5,9},{8,12},{9,13},{12,14},{13,15},{14,10},{15,... | collective-permute-start | bytes 1572872 | tf_op jit(solution)/shard_map/ppermute | solution.py:53
  113.4 14.5 %collective-permute-start.9 = (bf16[128,2048]{1,0:T(8,128)(2,1)}, bf16[128,2048]{1,0:T(8,128)(2,1)S(1)}, u32[]{:S(2)}, u32[]{:S(2)}) collective-permute-start(bf16[128,2048]{1,0:T(8,128)(2,1)} %collective-permute-done.8.refs_1_), channel_id=1, source_target_pairs={{0,2},{1,3},{4,0},{5,1},{8,4},{9,5},{12,8},{13,9},{14,12},{15,13},... | collective-permute-start | bytes 1572872 | tf_op jit(solution)/shard_map/ppermute | solution.py:53
  114.9 13.1 %collective-permute-start.18 = (bf16[128,2048]{1,0:T(8,128)(2,1)}, bf16[128,2048]{1,0:T(8,128)(2,1)S(1)}, u32[]{:S(2)}, u32[]{:S(2)}) collective-permute-start(bf16[128,2048]{1,0:T(8,128)(2,1)} %collective-permute-done.7.refs_1_), channel_id=1, source_target_pairs={{0,1},{1,0},{2,3},{3,2},{4,5},{5,4},{6,7},{7,6},{8,9},{9,8},{10,11... | collective-permute-start | bytes 1572872 | tf_op jit(solution)/shard_map/ppermute | solution.py:53
  116.5 11.6 %collective-permute-start.15 = (bf16[128,2048]{1,0:T(8,128)(2,1)}, bf16[128,2048]{1,0:T(8,128)(2,1)S(1)}, u32[]{:S(2)}, u32[]{:S(2)}) collective-permute-start(bf16[128,2048]{1,0:T(8,128)(2,1)} %collective-permute-done.4.refs_0_), channel_id=1, source_target_pairs={{0,1},{1,0},{2,3},{3,2},{4,5},{5,4},{6,7},{7,6},{8,9},{9,8},{10,11... | collective-permute-start | bytes 1572872 | tf_op jit(solution)/shard_map/ppermute | solution.py:53
  116.8 22.0 %collective-permute-start.16 = (bf16[128,2048]{1,0:T(8,128)(2,1)}, bf16[128,2048]{1,0:T(8,128)(2,1)S(1)}, u32[]{:S(2)}, u32[]{:S(2)}) collective-permute-start(bf16[128,2048]{1,0:T(8,128)(2,1)} %collective-permute-done.8.refs_1_), channel_id=1, source_target_pairs={{0,1},{1,0},{2,3},{3,2},{4,5},{5,4},{6,7},{7,6},{8,9},{9,8},{10,11... | collective-permute-start | bytes 1572872 | tf_op jit(solution)/shard_map/ppermute | solution.py:53
  126.1 18.7 %collective-permute-start.13 = (bf16[128,2048]{1,0:T(8,128)(2,1)S(1)}, bf16[128,2048]{1,0:T(8,128)(2,1)S(1)}, u32[]{:S(2)}, u32[]{:S(2)}) collective-permute-start(bf16[128,2048]{1,0:T(8,128)(2,1)S(1)} %collective-permute-done.5.refs_0_), channel_id=1, source_target_pairs={{0,1},{1,0},{2,3},{3,2},{4,5},{5,4},{6,7},{7,6},{8,9},{9,8},{10,11... | collective-permute-start | bytes 1572872 | tf_op jit(solution)/shard_map/ppermute | solution.py:53
  127.9 16.9 %collective-permute-start.14 = (bf16[128,2048]{1,0:T(8,128)(2,1)S(1)}, bf16[128,2048]{1,0:T(8,128)(2,1)S(1)}, u32[]{:S(2)}, u32[]{:S(2)}) collective-permute-start(bf16[128,2048]{1,0:T(8,128)(2,1)S(1)} %collective-permute-done.9.refs_1_), channel_id=1, source_target_pairs={{0,1},{1,0},{2,3},{3,2},{4,5},{5,4},{6,7},{7,6},{8,9},{9,8},{10,11... | collective-permute-start | bytes 1572872 | tf_op jit(solution)/shard_map/ppermute | solution.py:53
  128.0 15.9 %collective-permute-start.6 = (bf16[64,2048]{1,0:T(8,128)(2,1)S(1)}, bf16[64,2048]{1,0:T(8,128)(2,1)S(1)}, u32[]{:S(2)}, u32[]{:S(2)}) collective-permute-start(bf16[64,2048]{1,0:T(8,128)(2,1)S(1)} %slice.31), channel_id=1, source_target_pairs={{0,4},{1,5},{4,8},{5,9},{8,12},{9,13},{12,14},{13,15},{14,10},{15,... | collective-permute-start | bytes 786440 | tf_op jit(solution)/shard_map/ppermute | solution.py:53
  128.1 16.6 %collective-permute-start.10 = (bf16[64,2048]{1,0:T(8,128)(2,1)S(1)}, bf16[64,2048]{1,0:T(8,128)(2,1)S(1)}, u32[]{:S(2)}, u32[]{:S(2)}) collective-permute-start(bf16[64,2048]{1,0:T(8,128)(2,1)S(1)} %slice.32), channel_id=1, source_target_pairs={{0,2},{1,3},{4,0},{5,1},{8,4},{9,5},{12,8},{13,9},{14,12},{15,13},... | collective-permute-start | bytes 786440 | tf_op jit(solution)/shard_map/ppermute | solution.py:53
  143.9 6.5 %collective-permute-start.11 = (bf16[64,2048]{1,0:T(8,128)(2,1)S(1)}, bf16[64,2048]{1,0:T(8,128)(2,1)S(1)}, u32[]{:S(2)}, u32[]{:S(2)}) collective-permute-start(bf16[64,2048]{1,0:T(8,128)(2,1)S(1)} %collective-permute-done.6.refs_0_), channel_id=1, source_target_pairs={{0,1},{1,0},{2,3},{3,2},{4,5},{5,4},{6,7},{7,6},{8,9},{9,8},{10,11... | collective-permute-start | bytes 786440 | tf_op jit(solution)/shard_map/ppermute | solution.py:53
  144.7 5.7 %collective-permute-start.12 = (bf16[64,2048]{1,0:T(8,128)(2,1)S(1)}, bf16[64,2048]{1,0:T(8,128)(2,1)S(1)}, u32[]{:S(2)}, u32[]{:S(2)}) collective-permute-start(bf16[64,2048]{1,0:T(8,128)(2,1)S(1)} %collective-permute-done.10.refs_1_), channel_id=1, source_target_pairs={{0,1},{1,0},{2,3},{3,2},{4,5},{5,4},{6,7},{7,6},{8,9},{9,8},{10,11... | collective-permute-start | bytes 786440 | tf_op jit(solution)/shard_map/ppermute | solution.py:53
  (7 other events, 175.3 us)

commit v2 on v1

--- a/solution.py
+++ b/solution.py
@@ -231,7 +231,7 @@
             copy.wait()
 
 
-def last_stage(ids, at, hot_index, cols, table, rows, chunks, totals):
+def last_stage(ids, at, cols, table, rows, chunks, totals):
     group = len(chunks)
     arrays = [block for chunk in chunks for block in chunk]
     hidden = rows.shape[1]
@@ -260,7 +260,7 @@
         ),
         name="last_stage",
     )(
-        jnp.concatenate([ids, hot_index[None]]),
+        ids,
         cols,
         table,
         rows,
@@ -414,11 +414,11 @@
     )(in_vmem(chunk), in_vmem(hot), in_vmem(up_local), in_vmem(down_local))
 
 
-def back_body(count, piece_rows, piece_ref, *refs):
+def back_body(count, piece_ref, *refs):
     parts_in, out_ref = refs[:-1], refs[-1]
     rows = parts_in[0].shape[0]
-    width = out_ref.shape[1]
-    slots = 2 * HCAP + piece_rows
+    width = out_ref.shape[2]
+    slots = 2 * HCAP
     total = count * slots
     at = lax.broadcasted_iota(jnp.int32, (total, 1), 0)
     place, line = at // slots, at % slots
@@ -427,10 +427,9 @@
         within < CAP, place * CAP + within, count * CAP + place * EXTRA + within - CAP
     )
     outs = pick_rows(total, rows, jnp.where(line < HCAP, row, -1))
-    backs = pick_rows(
-        total, rows, jnp.where(jnp.logical_and(line >= HCAP, line < 2 * HCAP), row, -1)
-    )
-    pieces = pick_rows(total, piece_rows, line - 2 * HCAP)
+    backs = pick_rows(total, rows, jnp.where(line < HCAP, -1, row))
+    for k in range(count):
+        out_ref[k, slots:] = piece_ref[...]
 
     def summed(here):
         value = parts_in[0][:, here].astype(F32)
@@ -443,8 +442,9 @@
         here, there = pl.ds(start, block), pl.ds(width + start, block)
         value = jnp.dot(outs, summed(here), preferred_element_type=F32)
         value += jnp.dot(backs, summed(there), preferred_element_type=F32)
-        value += jnp.dot(pieces, piece_ref[:, here], preferred_element_type=F32)
-        out_ref[:, here] = value.astype(BF16)
+        value = value.astype(BF16)
+        for k in range(count):
+            out_ref[k, :slots, here] = value[k * slots : (k + 1) * slots]
 
 
 def back_rows(count, piece, parts_in):
@@ -452,10 +452,10 @@
     slots = 2 * HCAP + piece_rows
     vmem = pl.BlockSpec(memory_space=pltpu.VMEM)
     return pl.pallas_call(
-        functools.partial(back_body, count, piece_rows),
+        functools.partial(back_body, count),
         in_specs=[vmem] * (1 + len(parts_in)),
         out_specs=vmem,
-        out_shape=jax.ShapeDtypeStruct((count * slots, width), BF16),
+        out_shape=jax.ShapeDtypeStruct((count, slots, width), BF16),
         compiler_params=pltpu.CompilerParams(vmem_limit_bytes=24 * 2**20),
         cost_estimate=pl.CostEstimate(
             flops=8 * count * slots * parts_in[0].shape[0] * width,
@@ -463,7 +463,7 @@
             transcendentals=0,
         ),
         name="back_rows",
-    )(piece, *parts_in).reshape(count, slots, width)
+    )(piece, *parts_in)
 
 
 def combine_body(codes_ref, gates_ref, rows_ref, out_ref, back_ref):
@@ -604,6 +604,7 @@
     hot_index = jnp.sum(hot_mask * codes).astype(jnp.int32)
     owner = (hot_index == index).astype(jnp.int32)[None]
     sources = ring_sources(count)
+    last_ids = jnp.concatenate([sources, hot_index[None]])
 
     hot_extra = jnp.logical_and(
         expert_ids == hot_index, jnp.logical_and(route_slots >= CAP, route_slots < HCAP)
@@ -696,7 +697,7 @@
         axis=1,
     )
     grad_up, grad_down = last_stage(
-        sources, at, hot_index, cols, table, hot_rows, mine + others, totals
+        last_ids, at, cols, table, hot_rows, mine + others, totals
     )
     return (layer_out, grad_tokens, grad_up, grad_down)
 

time: 155 us -> 155 us (level)
  transfers between devices with their start and end apart: 23 -> 23, of which waited for: 4 -> 4; matrix products, arithmetic and copies ran while one was open for 4% -> 4% of each run, Pallas kernels for 24% -> 23%
where the time goes in v2:
time: 155 us; the launch traced here: 153 us
  waiting for transfers between devices  49 us (32%)
  Pallas kernels  41.3 us (27%)
  starting transfers between devices  31.6 us (20%)
  blocking collectives  19.9 us (13%)
  between operations  3.69 us (2%)
  local copies, waits for them, and re-layouts  3.66 us (2%)
  other arithmetic  2.82 us (2%)
    ppermute x17, waiting for transfers between devices, send(): return lax.ppermute(value, 'expert', pairs)  39 us
    all_to_all x1, blocking collectives, exchange(): lax.all_to_all(value, 'expert', split_axis=0, concat_axis=0, tiled=True)  19.9 us
    all_to_all x3, starting transfers between devices, exchange(): lax.all_to_all(value, 'expert', split_axis=0, concat_axis=0, tiled=True)  16.9 us
    pallas_call x4, Pallas kernels, grad_stage(): pl.pallas_call(functools.partial(grad_body, layout, first), grid_spec=plt...  16.6 us
    ppermute x17, starting transfers between devices, send(): return lax.ppermute(value, 'expert', pairs)  13 us
    all_to_all x3, waiting for transfers between devices, exchange(): lax.all_to_all(value, 'expert', split_axis=0, concat_axis=0, tiled=True)  9.94 us
    pallas_call x1, Pallas kernels, load(): pl.pallas_call(load_body, in_specs=[hbm, hbm], out_specs=[vmem, vmem], ou...  5.79 us
    pallas_call x1, Pallas kernels, ffn(): pl.pallas_call(functools.partial(ffn_body, planes, min(hidden, 256)), in_...  5.34 us
  transfers between devices with their start and end apart: 23, of which 4 were waited for; matrix products, arithmetic and copies ran while one was open for 4% of the time, Pallas kernels for 23%

profile of v2, /device:TPU:11, one launch (start us, length us, event | category | flops | bytes accessed | tf_op | source)
XLA Modules:
  0.0 153.1 jit_solution(17537092788899427903)
XLA Ops:
  1.3 2.5 %pack.1 = (bf16[128,2048]{1,0:T(8,128)(2,1)S(1)}, bf16[2,32,2048]{2,1,0:T(8,128)(2,1)S(1)}) custom-call(s32[16]{0:T(128)S(1)} %copy-done.2, s32[2,128]{1,0:T(2,128)} %bitcast.50, s32[2,128]{1,0:T(2,128)} %bitcast.49, f32[2,128]{1,0:T(2,128)} %bitcast.51, bf16[128,2048]{1,0:T(8,128)(2,1)} %refs_3_.1, bf16[128,2048]{1,0:T(8,128)(2,1)} %refs_4_.1), custom_call_target="tpu_custom_call" | custom-call | flops 201326592 | bytes 786432 | tf_op jit(solution)/shard_map/pack/pallas_call | solution.py:573
  3.8 19.9 %all_to_all.20 = bf16[16,8,2048]{2,1,0:T(8,128)(2,1)S(1)} all-to-all(bf16[16,8,2048]{2,1,0:T(8,128)(2,1)S(1)} %bitcast.41), channel_id=1, replica_groups=mesh['dp'=2,'expert'=16] {'expert'}, dimensions={0} | all-to-all | bytes 1048576 | tf_op jit(solution)/shard_map/all_to_all | solution.py:618
  25.8 5.1 %all-to-all-start.2 = ((bf16[16,32,256]{2,1,0:T(8,128)(2,1)}), bf16[16,32,256]{2,1,0:T(8,128)(2,1)S(1)}, u32[]{:S(2)}, u32[]{:S(2)}) async-start(bf16[16,32,256]{2,1,0:T(8,128)(2,1)} %maximum_bitcast_fusion), calls=%async_computation.2 | async-start | bytes 524288 | tf_op jit(solution)/shard_map/all_to_all | solution.py:618
  32.2 5.8 %load.1 = (bf16[2048,2048]{1,0:T(8,128)(2,1)S(1)}, bf16[2048,2048]{1,0:T(8,128)(2,1)S(1)}) custom-call(bf16[2048,2048]{1,0:T(8,128)(2,1)} %bitcast.42, bf16[2048,2048]{1,0:T(8,128)(2,1)} %bitcast.43), custom_call_target="tpu_custom_call" | custom-call | bytes 33554432 | tf_op jit(solution)/shard_map/load/pallas_call | solution.py:285
  38.0 5.3 %ffn.1 = (bf16[128,2048]{1,0:T(8,128)(2,1)S(1)}, bf16[128,2048]{1,0:T(8,128)(2,1)}) custom-call(s32[1]{0:T(128)} %bitcast.2.owner_ref, bf16[128,2048]{1,0:T(8,128)(2,1)S(1)} %bitcast.39, bf16[128,2048]{1,0:T(8,128)(2,1)S(1)} %collective-permute-done.refs_1_, bf16[2048,2048]{1,0:T(8,128)(2,1)S(1)} %get-tuple-element.28.refs_2_.up_ref, ...), custom_call_target="tpu_custom_call" | custom-call | flops 2147483648 | bytes 16777216 | tf_op jit(solution)/shard_map/ffn/pallas_call | solution.py:353
  43.4 5.0 %parts.1 = bf16[2,64,4096]{2,1,0:T(8,128)(2,1)S(1)} custom-call(bf16[128,2048]{1,0:T(8,128)(2,1)S(1)} %get-tuple-element.31.chunk_ref.refs_0_, bf16[128,2048]{1,0:T(8,128)(2,1)} %get-tuple-element.30.hot_ref, bf16[2048,2048]{1,0:T(8,128)(2,1)S(1)} %get-tuple-element.28.refs_2_.up_ref, bf16[2048,2048]{1,0:T(8,128)(2,1)S(1)} %get-tuple-element.29.refs_3_.down_ref), custom_call_target="tpu_custom_call" | custom-call | flops 2147483648 | bytes 16777216 | tf_op jit(solution)/shard_map/parts/pallas_call | solution.py:401
  48.5 6.0 %all-to-all-start.1 = ((bf16[16,8,2048]{2,1,0:T(8,128)(2,1)}), bf16[16,8,2048]{2,1,0:T(8,128)(2,1)}, u32[]{:S(2)}, u32[]{:S(2)}) async-start(bf16[16,8,2048]{2,1,0:T(8,128)(2,1)} %bitcast.9), calls=%async_computation.1 | async-start | bytes 1048576 | tf_op jit(solution)/shard_map/all_to_all | solution.py:618
  59.1 9.9 %all-to-all-done.1 = bf16[16,8,2048]{2,1,0:T(8,128)(2,1)} async-done(((bf16[16,8,2048]{2,1,0:T(8,128)(2,1)}), bf16[16,8,2048]{2,1,0:T(8,128)(2,1)}, u32[]{:S(2)}, u32[]{:S(2)}) %all-to-all-start.1) | async-done | bytes 524320 | tf_op jit(solution)/shard_map/all_to_all | solution.py:618
  69.8 1.4 back_rows.1
  71.2 5.7 %all-to-all-start.3 = ((bf16[16,16,2048]{2,1,0:T(8,128)(2,1)}), bf16[16,16,2048]{2,1,0:T(8,128)(2,1)S(1)}, u32[]{:S(2)}, u32[]{:S(2)}) async-start(bf16[16,16,2048]{2,1,0:T(8,128)(2,1)} %back_rows.1), calls=%async_computation.3 | async-start | bytes 2097152 | tf_op jit(solution)/shard_map/all_to_all | solution.py:618
  79.0 1.5 collective-permute-start.8
  80.6 1.6 %collective-permute-start.19 = (bf16[128,2048]{1,0:T(8,128)(2,1)S(1)}, bf16[128,2048]{1,0:T(8,128)(2,1)S(1)}, u32[]{:S(2)}, u32[]{:S(2)}) collective-permute-start(bf16[128,2048]{1,0:T(8,128)(2,1)S(1)} %get-tuple-element.31.chunk_ref.refs_0_), channel_id=1, source_target_pairs={{0,1},{1,0},{2,3},{3,2},{4,5},{5,4},{6,7},{7,6},{8,9},{9,8},{10,11... | collective-permute-start | bytes 1572872 | tf_op jit(solution)/shard_map/ppermute | solution.py:53
  83.8 29.1 %collective-permute-done.4.refs_0_ = bf16[128,2048]{1,0:T(8,128)(2,1)} collective-permute-done((bf16[128,2048]{1,0:T(8,128)(2,1)S(1)}, bf16[128,2048]{1,0:T(8,128)(2,1)}, u32[]{:S(2)}, u32[]{:S(2)}) %collective-permute-start.4) | collective-permute-done | bytes 524320 | tf_op jit(solution)/shard_map/ppermute | solution.py:53
  112.9 1.5 collective-permute-start.9
  114.4 1.6 %collective-permute-start.18 = (bf16[128,2048]{1,0:T(8,128)(2,1)}, bf16[128,2048]{1,0:T(8,128)(2,1)S(1)}, u32[]{:S(2)}, u32[]{:S(2)}) collective-permute-start(bf16[128,2048]{1,0:T(8,128)(2,1)} %collective-permute-done.7.refs_1_), channel_id=1, source_target_pairs={{0,1},{1,0},{2,3},{3,2},{4,5},{5,4},{6,7},{7,6},{8,9},{9,8},{10,11... | collective-permute-start | bytes 1572872 | tf_op jit(solution)/shard_map/ppermute | solution.py:53
  117.0 8.6 %collective-permute-done.5.refs_0_ = bf16[128,2048]{1,0:T(8,128)(2,1)S(1)} collective-permute-done((bf16[128,2048]{1,0:T(8,128)(2,1)}, bf16[128,2048]{1,0:T(8,128)(2,1)S(1)}, u32[]{:S(2)}, u32[]{:S(2)}) %collective-permute-start.5) | collective-permute-done | bytes 524320 | tf_op jit(solution)/shard_map/ppermute | solution.py:53
  125.6 1.8 %collective-permute-start.13 = (bf16[128,2048]{1,0:T(8,128)(2,1)S(1)}, bf16[128,2048]{1,0:T(8,128)(2,1)S(1)}, u32[]{:S(2)}, u32[]{:S(2)}) collective-permute-start(bf16[128,2048]{1,0:T(8,128)(2,1)S(1)} %collective-permute-done.5.refs_0_), channel_id=1, source_target_pairs={{0,1},{1,0},{2,3},{3,2},{4,5},{5,4},{6,7},{7,6},{8,9},{9,8},{10,11... | collective-permute-start | bytes 1572872 | tf_op jit(solution)/shard_map/ppermute | solution.py:53
  127.6 1.7 %collective-permute-start.10 = (bf16[64,2048]{1,0:T(8,128)(2,1)S(1)}, bf16[64,2048]{1,0:T(8,128)(2,1)S(1)}, u32[]{:S(2)}, u32[]{:S(2)}) collective-permute-start(bf16[64,2048]{1,0:T(8,128)(2,1)S(1)} %slice.32), channel_id=1, source_target_pairs={{0,2},{1,3},{4,0},{5,1},{8,4},{9,5},{12,8},{13,9},{14,12},{15,13},... | collective-permute-start | bytes 786440 | tf_op jit(solution)/shard_map/ppermute | solution.py:53
  129.7 2.5 %grad_stage.4 = (bf16[16,128,2048]{2,1,0:T(8,128)(2,1)}, bf16[16,128,2048]{2,1,0:T(8,128)(2,1)}) custom-call(s32[16]{0:T(128)S(1)} %fusion.22.ids_ref, bf16[16,64,256]{2,1,0:T(8,128)(2,1)S(1)} %pad_maximum_fusion.cols_ref, bf16[128,2048]{1,0:T(8,128)(2,1)S(1)} %get-tuple-element.31.chunk_ref.refs_0_, bf16[128,2048]{1,0:T(8,128)(2,1)S(1)} %collective-permute-done.19.refs_1_), custom_call_target="tpu_custom_call" | custom-call | flops 134217728 | bytes 3145728 | tf_op jit(solution)/shard_map/grad_stage/pallas_call | solution.py:150
  133.2 5.0 %grad_stage.5 = (bf16[16,128,2048]{2,1,0:T(8,128)(2,1)}, bf16[16,128,2048]{2,1,0:T(8,128)(2,1)}) custom-call(s32[16]{0:T(128)S(1)} %fusion.22.ids_ref, bf16[16,64,256]{2,1,0:T(8,128)(2,1)S(1)} %pad_maximum_fusion.cols_ref, bf16[128,2048]{1,0:T(8,128)(2,1)S(1)} %copy-done.1, ...), custom_call_target="tpu_custom_call", output_to_operand_aliasing={{0}: (6, {}), {1}: (7, {})} | custom-call | flops 268435456 | bytes 6291456 | tf_op jit(solution)/shard_map/grad_stage/pallas_call | solution.py:150
  138.2 5.2 %grad_stage.6 = (bf16[16,128,2048]{2,1,0:T(8,128)(2,1)}, bf16[16,128,2048]{2,1,0:T(8,128)(2,1)}) custom-call(s32[16]{0:T(128)S(1)} %fusion.22.ids_ref, bf16[16,64,256]{2,1,0:T(8,128)(2,1)S(1)} %pad_maximum_fusion.cols_ref, bf16[128,2048]{1,0:T(8,128)(2,1)} %collective-permute-done.4.refs_0_, ...), custom_call_target="tpu_custom_call", output_to_operand_aliasing={{0}: (6, {}), {1}: (7, {})} | custom-call | flops 268435456 | bytes 6291456 | tf_op jit(solution)/shard_map/grad_stage/pallas_call | solution.py:150
  144.3 4.0 %grad_stage.7 = (bf16[16,128,2048]{2,1,0:T(8,128)(2,1)}, bf16[16,128,2048]{2,1,0:T(8,128)(2,1)}) custom-call(s32[16]{0:T(128)S(1)} %fusion.22.ids_ref, bf16[16,64,256]{2,1,0:T(8,128)(2,1)S(1)} %pad_maximum_fusion.cols_ref, bf16[128,2048]{1,0:T(8,128)(2,1)S(1)} %collective-permute-done.5.refs_0_, ...), custom_call_target="tpu_custom_call", output_to_operand_aliasing={{0}: (6, {}), {1}: (7, {})} | custom-call | flops 268435456 | bytes 6291456 | tf_op jit(solution)/shard_map/grad_stage/pallas_call | solution.py:150
  148.2 1.6 %combine.1 = (bf16[128,2048]{1,0:T(8,128)(2,1)}, bf16[128,2048]{1,0:T(8,128)(2,1)}) custom-call(s32[8,128]{1,0:T(8,128)S(1)} %pad.10.codes_ref, f32[8,128]{1,0:T(8,128)S(1)} %pad.11.gates_ref, bf16[256,2048]{1,0:T(8,128)(2,1)S(1)} %bitcast.37), custom_call_target="tpu_custom_call" | custom-call | flops 402653184 | bytes 3145728 | tf_op jit(solution)/shard_map/combine/pallas_call | solution.py:497
  149.9 3.0 %last_stage.1 = (bf16[16,128,2048]{2,1,0:T(8,128)(2,1)}, bf16[16,128,2048]{2,1,0:T(8,128)(2,1)}) custom-call(s32[17]{0:T(128)S(1)} %pad_add_fusion.ids_ref, bf16[16,64,256]{2,1,0:T(8,128)(2,1)S(1)} %pad_maximum_fusion.cols_ref, bf16[128,256]{1,0:T(8,128)(2,1)S(1)} %pad_maximum_fusion.2.table_ref, ...), custom_call_target="tpu_custom_call", output_to_operand_aliasing={{0}: (8, {}), {1}: (9, {})} | custom-call | flops 1073741824 | bytes 4194304 | tf_op jit(solution)/shard_map/last_stage/pallas_call | solution.py:242
  (78 shorter events, 14.1 us)
Async XLA Ops:
  23.7 14.4 %collective-permute-start = (bf16[128,2048]{1,0:T(8,128)(2,1)S(1)}, bf16[128,2048]{1,0:T(8,128)(2,1)S(1)}, u32[]{:S(2)}, u32[]{:S(2)}) collective-permute-start(bf16[128,2048]{1,0:T(8,128)(2,1)S(1)} %bitcast.38), channel_id=1, source_target_pairs={{0,16},{16,0},{1,17},{17,1},{2,18},{18,2},{3,19},{19,3},{4,20},{20... | collective-permute-start | bytes 1572872 | tf_op jit(solution)/shard_map/ppermute | solution.py:58
  25.8 22.7 %all-to-all-start.2 = ((bf16[16,32,256]{2,1,0:T(8,128)(2,1)}), bf16[16,32,256]{2,1,0:T(8,128)(2,1)S(1)}, u32[]{:S(2)}, u32[]{:S(2)}) async-start(bf16[16,32,256]{2,1,0:T(8,128)(2,1)} %maximum_bitcast_fusion), calls=%async_computation.2 | async-start | bytes 524288 | tf_op jit(solution)/shard_map/all_to_all | solution.py:618
  48.5 20.5 %all-to-all-start.1 = ((bf16[16,8,2048]{2,1,0:T(8,128)(2,1)}), bf16[16,8,2048]{2,1,0:T(8,128)(2,1)}, u32[]{:S(2)}, u32[]{:S(2)}) async-start(bf16[16,8,2048]{2,1,0:T(8,128)(2,1)} %bitcast.9), calls=%async_computation.1 | async-start | bytes 1048576 | tf_op jit(solution)/shard_map/all_to_all | solution.py:618
  55.3 14.4 %collective-permute-start.1 = (bf16[64,4096]{1,0:T(8,128)(2,1)}, bf16[64,4096]{1,0:T(8,128)(2,1)S(1)}, u32[]{:S(2)}, u32[]{:S(2)}) collective-permute-start(bf16[64,4096]{1,0:T(8,128)(2,1)} %get-tuple-element.50), channel_id=1, source_target_pairs={{0,16},{16,0},{1,17},{17,1},{2,18},{18,2},{3,19},{19,3},{4,20},{20... | collective-permute-start | bytes 1572872 | tf_op jit(solution)/shard_map/ppermute | solution.py:58
  57.5 21.4 %collective-permute-start.3 = (bf16[128,2048]{1,0:T(8,128)(2,1)S(1)}, bf16[128,2048]{1,0:T(8,128)(2,1)S(1)}, u32[]{:S(2)}, u32[]{:S(2)}) collective-permute-start(bf16[128,2048]{1,0:T(8,128)(2,1)S(1)} %get-tuple-element.31.chunk_ref.refs_0_), channel_id=1, source_target_pairs={{0,4},{1,5},{4,8},{5,9},{8,12},{9,13},{12,14},{13,15},{14,10},{15,... | collective-permute-start | bytes 1572872 | tf_op jit(solution)/shard_map/ppermute | solution.py:53
  57.9 21.1 %collective-permute-start.7 = (bf16[128,2048]{1,0:T(8,128)(2,1)S(1)}, bf16[128,2048]{1,0:T(8,128)(2,1)}, u32[]{:S(2)}, u32[]{:S(2)}) collective-permute-start(bf16[128,2048]{1,0:T(8,128)(2,1)S(1)} %get-tuple-element.31.chunk_ref.refs_0_), channel_id=1, source_target_pairs={{0,2},{1,3},{4,0},{5,1},{8,4},{9,5},{12,8},{13,9},{14,12},{15,13},... | collective-permute-start | bytes 1572872 | tf_op jit(solution)/shard_map/ppermute | solution.py:53
  71.2 77.0 %all-to-all-start.3 = ((bf16[16,16,2048]{2,1,0:T(8,128)(2,1)}), bf16[16,16,2048]{2,1,0:T(8,128)(2,1)S(1)}, u32[]{:S(2)}, u32[]{:S(2)}) async-start(bf16[16,16,2048]{2,1,0:T(8,128)(2,1)} %back_rows.1), calls=%async_computation.3 | async-start | bytes 2097152 | tf_op jit(solution)/shard_map/all_to_all | solution.py:618
  79.0 50.7 %copy-start = (bf16[128,2048]{1,0:T(8,128)(2,1)}, bf16[128,2048]{1,0:T(8,128)(2,1)S(1)}, u32[]{:S(2)}) copy-start(bf16[128,2048]{1,0:T(8,128)(2,1)S(1)} %collective-permute-done.3.refs_0_) | copy-start | bytes 1572868
  79.0 33.9 %collective-permute-start.4 = (bf16[128,2048]{1,0:T(8,128)(2,1)S(1)}, bf16[128,2048]{1,0:T(8,128)(2,1)}, u32[]{:S(2)}, u32[]{:S(2)}) collective-permute-start(bf16[128,2048]{1,0:T(8,128)(2,1)S(1)} %collective-permute-done.3.refs_0_), channel_id=1, source_target_pairs={{0,4},{1,5},{4,8},{5,9},{8,12},{9,13},{12,14},{13,15},{14,10},{15,... | collective-permute-start | bytes 1572872 | tf_op jit(solution)/shard_map/ppermute | solution.py:53
  79.0 33.9 %collective-permute-start.8 = (bf16[128,2048]{1,0:T(8,128)(2,1)}, bf16[128,2048]{1,0:T(8,128)(2,1)}, u32[]{:S(2)}, u32[]{:S(2)}) collective-permute-start(bf16[128,2048]{1,0:T(8,128)(2,1)} %collective-permute-done.7.refs_1_), channel_id=1, source_target_pairs={{0,2},{1,3},{4,0},{5,1},{8,4},{9,5},{12,8},{13,9},{14,12},{15,13},... | collective-permute-start | bytes 1572872 | tf_op jit(solution)/shard_map/ppermute | solution.py:53
  80.6 35.4 %collective-permute-start.19 = (bf16[128,2048]{1,0:T(8,128)(2,1)S(1)}, bf16[128,2048]{1,0:T(8,128)(2,1)S(1)}, u32[]{:S(2)}, u32[]{:S(2)}) collective-permute-start(bf16[128,2048]{1,0:T(8,128)(2,1)S(1)} %get-tuple-element.31.chunk_ref.refs_0_), channel_id=1, source_target_pairs={{0,1},{1,0},{2,3},{3,2},{4,5},{5,4},{6,7},{7,6},{8,9},{9,8},{10,11... | collective-permute-start | bytes 1572872 | tf_op jit(solution)/shard_map/ppermute | solution.py:53
  82.9 31.5 %collective-permute-start.2 = (bf16[16,32,256]{2,1,0:T(8,128)(2,1)S(1)}, bf16[16,32,256]{2,1,0:T(8,128)(2,1)S(1)}, u32[]{:S(2)}, u32[]{:S(2)}) collective-permute-start(bf16[16,32,256]{2,1,0:T(8,128)(2,1)S(1)} %all-to-all-done.2), channel_id=1, source_target_pairs={{0,16},{16,0},{1,17},{17,1},{2,18},{18,2},{3,19},{19,3},{4,20},{20... | collective-permute-start | bytes 786440 | tf_op jit(solution)/shard_map/ppermute | solution.py:58
  83.1 33.1 %collective-permute-start.17 = (bf16[128,2048]{1,0:T(8,128)(2,1)S(1)}, bf16[128,2048]{1,0:T(8,128)(2,1)S(1)}, u32[]{:S(2)}, u32[]{:S(2)}) collective-permute-start(bf16[128,2048]{1,0:T(8,128)(2,1)S(1)} %collective-permute-done.3.refs_0_), channel_id=1, source_target_pairs={{0,1},{1,0},{2,3},{3,2},{4,5},{5,4},{6,7},{7,6},{8,9},{9,8},{10,11... | collective-permute-start | bytes 1572872 | tf_op jit(solution)/shard_map/ppermute | solution.py:53
  112.9 12.7 %collective-permute-start.5 = (bf16[128,2048]{1,0:T(8,128)(2,1)}, bf16[128,2048]{1,0:T(8,128)(2,1)S(1)}, u32[]{:S(2)}, u32[]{:S(2)}) collective-permute-start(bf16[128,2048]{1,0:T(8,128)(2,1)} %collective-permute-done.4.refs_0_), channel_id=1, source_target_pairs={{0,4},{1,5},{4,8},{5,9},{8,12},{9,13},{12,14},{13,15},{14,10},{15,... | collective-permute-start | bytes 1572872 | tf_op jit(solution)/shard_map/ppermute | solution.py:53
  112.9 14.5 %collective-permute-start.9 = (bf16[128,2048]{1,0:T(8,128)(2,1)}, bf16[128,2048]{1,0:T(8,128)(2,1)S(1)}, u32[]{:S(2)}, u32[]{:S(2)}) collective-permute-start(bf16[128,2048]{1,0:T(8,128)(2,1)} %collective-permute-done.8.refs_1_), channel_id=1, source_target_pairs={{0,2},{1,3},{4,0},{5,1},{8,4},{9,5},{12,8},{13,9},{14,12},{15,13},... | collective-permute-start | bytes 1572872 | tf_op jit(solution)/shard_map/ppermute | solution.py:53
  114.4 13.1 %collective-permute-start.18 = (bf16[128,2048]{1,0:T(8,128)(2,1)}, bf16[128,2048]{1,0:T(8,128)(2,1)S(1)}, u32[]{:S(2)}, u32[]{:S(2)}) collective-permute-start(bf16[128,2048]{1,0:T(8,128)(2,1)} %collective-permute-done.7.refs_1_), channel_id=1, source_target_pairs={{0,1},{1,0},{2,3},{3,2},{4,5},{5,4},{6,7},{7,6},{8,9},{9,8},{10,11... | collective-permute-start | bytes 1572872 | tf_op jit(solution)/shard_map/ppermute | solution.py:53
  116.0 11.6 %collective-permute-start.15 = (bf16[128,2048]{1,0:T(8,128)(2,1)}, bf16[128,2048]{1,0:T(8,128)(2,1)S(1)}, u32[]{:S(2)}, u32[]{:S(2)}) collective-permute-start(bf16[128,2048]{1,0:T(8,128)(2,1)} %collective-permute-done.4.refs_0_), channel_id=1, source_target_pairs={{0,1},{1,0},{2,3},{3,2},{4,5},{5,4},{6,7},{7,6},{8,9},{9,8},{10,11... | collective-permute-start | bytes 1572872 | tf_op jit(solution)/shard_map/ppermute | solution.py:53
  116.3 21.9 %collective-permute-start.16 = (bf16[128,2048]{1,0:T(8,128)(2,1)}, bf16[128,2048]{1,0:T(8,128)(2,1)S(1)}, u32[]{:S(2)}, u32[]{:S(2)}) collective-permute-start(bf16[128,2048]{1,0:T(8,128)(2,1)} %collective-permute-done.8.refs_1_), channel_id=1, source_target_pairs={{0,1},{1,0},{2,3},{3,2},{4,5},{5,4},{6,7},{7,6},{8,9},{9,8},{10,11... | collective-permute-start | bytes 1572872 | tf_op jit(solution)/shard_map/ppermute | solution.py:53
  125.6 18.7 %collective-permute-start.13 = (bf16[128,2048]{1,0:T(8,128)(2,1)S(1)}, bf16[128,2048]{1,0:T(8,128)(2,1)S(1)}, u32[]{:S(2)}, u32[]{:S(2)}) collective-permute-start(bf16[128,2048]{1,0:T(8,128)(2,1)S(1)} %collective-permute-done.5.refs_0_), channel_id=1, source_target_pairs={{0,1},{1,0},{2,3},{3,2},{4,5},{5,4},{6,7},{7,6},{8,9},{9,8},{10,11... | collective-permute-start | bytes 1572872 | tf_op jit(solution)/shard_map/ppermute | solution.py:53
  127.4 16.9 %collective-permute-start.14 = (bf16[128,2048]{1,0:T(8,128)(2,1)S(1)}, bf16[128,2048]{1,0:T(8,128)(2,1)S(1)}, u32[]{:S(2)}, u32[]{:S(2)}) collective-permute-start(bf16[128,2048]{1,0:T(8,128)(2,1)S(1)} %collective-permute-done.9.refs_1_), channel_id=1, source_target_pairs={{0,1},{1,0},{2,3},{3,2},{4,5},{5,4},{6,7},{7,6},{8,9},{9,8},{10,11... | collective-permute-start | bytes 1572872 | tf_op jit(solution)/shard_map/ppermute | solution.py:53
  127.5 15.9 %collective-permute-start.6 = (bf16[64,2048]{1,0:T(8,128)(2,1)S(1)}, bf16[64,2048]{1,0:T(8,128)(2,1)S(1)}, u32[]{:S(2)}, u32[]{:S(2)}) collective-permute-start(bf16[64,2048]{1,0:T(8,128)(2,1)S(1)} %slice.31), channel_id=1, source_target_pairs={{0,4},{1,5},{4,8},{5,9},{8,12},{9,13},{12,14},{13,15},{14,10},{15,... | collective-permute-start | bytes 786440 | tf_op jit(solution)/shard_map/ppermute | solution.py:53
  127.6 16.6 %collective-permute-start.10 = (bf16[64,2048]{1,0:T(8,128)(2,1)S(1)}, bf16[64,2048]{1,0:T(8,128)(2,1)S(1)}, u32[]{:S(2)}, u32[]{:S(2)}) collective-permute-start(bf16[64,2048]{1,0:T(8,128)(2,1)S(1)} %slice.32), channel_id=1, source_target_pairs={{0,2},{1,3},{4,0},{5,1},{8,4},{9,5},{12,8},{13,9},{14,12},{15,13},... | collective-permute-start | bytes 786440 | tf_op jit(solution)/shard_map/ppermute | solution.py:53
  143.4 6.5 %collective-permute-start.11 = (bf16[64,2048]{1,0:T(8,128)(2,1)S(1)}, bf16[64,2048]{1,0:T(8,128)(2,1)S(1)}, u32[]{:S(2)}, u32[]{:S(2)}) collective-permute-start(bf16[64,2048]{1,0:T(8,128)(2,1)S(1)} %collective-permute-done.6.refs_0_), channel_id=1, source_target_pairs={{0,1},{1,0},{2,3},{3,2},{4,5},{5,4},{6,7},{7,6},{8,9},{9,8},{10,11... | collective-permute-start | bytes 786440 | tf_op jit(solution)/shard_map/ppermute | solution.py:53
  144.2 5.7 %collective-permute-start.12 = (bf16[64,2048]{1,0:T(8,128)(2,1)S(1)}, bf16[64,2048]{1,0:T(8,128)(2,1)S(1)}, u32[]{:S(2)}, u32[]{:S(2)}) collective-permute-start(bf16[64,2048]{1,0:T(8,128)(2,1)S(1)} %collective-permute-done.10.refs_1_), channel_id=1, source_target_pairs={{0,1},{1,0},{2,3},{3,2},{4,5},{5,4},{6,7},{7,6},{8,9},{9,8},{10,11... | collective-permute-start | bytes 786440 | tf_op jit(solution)/shard_map/ppermute | solution.py:53
  (7 other events, 173.3 us)
